TPU v7x, 32 devices: a whole 2x2x4 slice. The times are simulated.
32 devices in a mesh: feed: 8 (over y, x, core), tm: 4 (over z).
Axes of the slice: x: 2, y: 2, z: 4, core: 2. Of those that a mesh axis runs over, the one named last changes fastest.
Arguments:
- voltages: bfloat16 [256, 1048576], P('feed', 'tm'), may hold values from -12 to 12
- filter_taps: float32 [4, 1024], replicated, may hold values from -1 to 1
- delays: float32 [256], P('feed'), may hold values from -64 to 64
- channel_flags: int32 [512], P('feed'), may hold values from 0 to 1, as said below
Outputs:
- visibilities: float32 [512, 256, 256], P(('feed', 'tm'))
Inputs may be any that keep to these rules, and one draw needn't show every extreme that they name: `channel_flags`: channel c belongs to owner c // 64; every owner keeps between 16 and 64 of its channels, and in every draw some owner keeps all of them.
All inputs are finite; a program needn't handle non-finite values.
Results may differ from a plain program's by a relative error of at most 0.0011.
Values may be sent and summed in bfloat16 or wider, within the bound.
A program may use at most 192 MiB of HBM per device.

v0:
```python
import math

import jax
import jax.numpy as jnp
from jax import lax
from jax.sharding import PartitionSpec as P


def passed_along(block, axis, distance):
    devices = range(lax.axis_size(axis))
    route = [(i - distance, i) for i in devices if i - distance in devices]
    return lax.ppermute(block, axis, route)


def build_table(fft_length):
    channels = jnp.arange(fft_length // 2, dtype=jnp.int32)
    samples = jnp.arange(fft_length, dtype=jnp.int32)
    product = channels[:, None] * samples[None, :] % fft_length
    angles = product.astype(jnp.float32) * (2.0 * math.pi / fft_length)
    return jnp.stack([jnp.cos(angles), -jnp.sin(angles)], axis=1).astype(jnp.bfloat16)


def rotate_phase(real_part, imag_part, channels, delay_values, fft_length):
    angles = 2.0 * math.pi / fft_length * channels * delay_values
    cosine = jnp.cos(angles)
    sine_part = jnp.sin(angles)
    factor = 1.0 / math.sqrt(fft_length)
    return (
        (real_part * cosine + imag_part * sine_part) * factor,
        (imag_part * cosine - real_part * sine_part) * factor,
    )


def gram_blocks(turned, local_frame_count, frame_total):
    count_here, inputs_all, columns = turned.shape
    split = turned.reshape(
        count_here, inputs_all, columns // (2 * local_frame_count), 2, local_frame_count
    )
    real_half = split[:, :, :, 0].reshape(count_here, inputs_all, columns // 2)
    imag_half = split[:, :, :, 1].reshape(count_here, inputs_all, columns // 2)
    block_rows = min(128, inputs_all)
    column_index = jnp.arange(inputs_all)[None, :]
    row_blocks = []
    for first in range(0, inputs_all, block_rows):
        last = first + block_rows
        upper = jnp.einsum(
            "cik,cjk->cij",
            turned[:, first:last],
            turned[:, first:],
            preferred_element_type=jnp.float32,
        )
        lower = jnp.einsum(
            "cik,cjk->cij",
            imag_half[:, first:last],
            real_half[:, :last],
            preferred_element_type=jnp.float32,
        )
        lower = lower - jnp.einsum(
            "cik,cjk->cij",
            real_half[:, first:last],
            imag_half[:, :last],
            preferred_element_type=jnp.float32,
        )
        upper_full = jnp.pad(upper, ((0, 0), (0, 0), (first, 0)))
        lower_full = jnp.pad(lower, ((0, 0), (0, 0), (0, inputs_all - last)))
        row_index = jnp.arange(first, last)[:, None]
        row_blocks.append(jnp.where(row_index <= column_index, upper_full, lower_full))
    return jnp.concatenate(row_blocks, axis=1) / frame_total


def on_device(voltages, filter_taps, delays, channel_flags):
    inputs_here, sample_count = voltages.shape
    tap_count, fft_length = filter_taps.shape
    local_frame_count = sample_count // fft_length
    frames = voltages.reshape(inputs_here, local_frame_count, fft_length)
    history = passed_along(frames[:, local_frame_count - (tap_count - 1) :, :], "tm", 1)
    extended = jnp.concatenate([history, frames], axis=1).astype(jnp.float32)
    filtered = filter_taps[0] * extended[:, tap_count - 1 : tap_count - 1 + local_frame_count]
    for tap_index in range(1, tap_count):
        offset = tap_count - 1 - tap_index
        filtered = (
            filtered + filter_taps[tap_index] * extended[:, offset : offset + local_frame_count]
        )
    filtered = filtered.astype(jnp.bfloat16)
    dft_table = build_table(fft_length)
    raw_spectra = jnp.einsum(
        "cpn,isn->cips", dft_table, filtered, preferred_element_type=jnp.float32
    )
    channels = jnp.arange(fft_length // 2).astype(jnp.float32)[:, None, None]
    real_part, imag_part = rotate_phase(
        raw_spectra[:, :, 0], raw_spectra[:, :, 1], channels, delays[None, :, None], fft_length
    )
    spectra = jnp.concatenate([real_part, imag_part], axis=2).astype(jnp.bfloat16)
    time_devices = lax.axis_size("tm")
    frame_total = local_frame_count * time_devices
    channels_here = channel_flags.shape[0] // time_devices
    local_flags = lax.dynamic_slice_in_dim(
        channel_flags, lax.axis_index("tm") * channels_here, channels_here, 0
    )
    turned = lax.all_to_all(spectra, "feed", split_axis=0, concat_axis=1, tiled=True)
    visibility = lax.psum_scatter(
        gram_blocks(turned, local_frame_count, frame_total), "tm", scatter_dimension=0, tiled=True
    )
    return visibility * local_flags[:, None, None].astype(jnp.float32)


def solution(mesh):
    in_specs = (P("feed", "tm"), P(), P("feed"), P("feed"))
    out_specs = P(("feed", "tm"), None, None)
    return jax.shard_map(
        on_device, mesh=mesh, in_specs=in_specs, out_specs=out_specs, check_vma=False
    )
```

profile of v0, /device:TPU:18, one launch (start us, length us, event | category | flops | bytes accessed | tf_op | source)
XLA Modules:
  0.0 796.2 jit_solution(467650899731393742)
XLA Ops:
  6.5 15.4 %copy.23 = bf16[4,8,256,1024]{3,2,1,0:T(8,128)(2,1)S(1)} copy(bf16[4,8,256,1024]{3,1,2,0:T(8,128)(2,1)} %bitcast.67) | data formatting | bytes 33554432
  22.1 3.5 collective-permute-start
  25.6 8.5 %negate_convert_fusion = (bf16[512,1,1024]{2,0,1:T(8,128)(2,1)S(1)}, bf16[512,1,1024]{2,0,1:T(8,128)(2,1)S(1)}) fusion(), kind=kLoop, calls=%fused_computation.49 | loop fusion | flops 8912896 | bytes 2097152 | tf_op jit(solution)/shard_map/convert.3
  34.5 12.0 %maximum_convert_fusion = f32[32,259,1024]{2,1,0:T(8,128)} fusion(bf16[32,256,1024]{2,1,0:T(8,128)(2,1)S(1)} %bitcast.66, bf16[32,3,1024]{2,1,0:T(4,128)(2,1)S(1)} %collective-permute-done), kind=kLoop, calls=%fused_computation.8 | loop fusion | flops 33947648 | bytes 50921472 | tf_op jit(solution)/shard_map/convert_element_type | solution.py:77
  46.4 56.9 %fusion.10 = f32[512,32,2,256]{0,3,2,1:T(8,128)} fusion(f32[32,259,1024]{2,1,0:T(8,128)} %maximum_convert_fusion, f32[1024]{0:T(1024)S(1)} %bitcast.70, f32[1024]{0:T(1024)S(1)} %bitcast.71, f32[1024]{0:T(1024)S(1)} %bitcast.69, f32[1024]{0:T(1024)S(1)} %bitcast.68, bf16[512,1,1024]{2,0,1:T(8,128)(2,1)S(1)} %get-tuple-element.15, ...), kind=kOutput, calls=%fused_computation.20 | convolution fusion | flops 17251172352 | bytes 169885696 | tf_op jit(solution)/shard_map/cpn,isn->cips/dot_general | solution.py:86
  103.4 12.3 %multiply_convert_fusion.1 = (bf16[512,32,256]{0,2,1:T(8,128)(2,1)S(1)}, bf16[512,32,256]{0,2,1:T(8,128)(2,1)S(1)}) fusion(f32[512,32,2,256]{0,3,2,1:T(8,128)} %fusion.10, f32[512,32]{0,1:T(8,128)S(1)} %get-tuple-element.14, f32[512,32]{0,1:T(8,128)S(1)} %get-tuple-element.13), kind=kLoop, calls=%fused_computation.16 | loop fusion | flops 41943040 | bytes 50462720 | tf_op jit(solution)/shard_map/convert
  115.6 6.5 pad_maximum_fusion
  122.2 28.6 %copy.14 = bf16[512,32,512]{2,1,0:T(8,128)(2,1)} copy(bf16[512,32,512]{0,2,1:T(8,128)(2,1)} %pad_maximum_fusion) | data formatting | bytes 33554432 | tf_op jit(solution)/shard_map/concatenate | solution.py:93
  150.8 6.1 all-to-all-start
  157.0 182.4 %all-to-all-done = bf16[512,32,512]{2,1,0:T(8,128)(2,1)} async-done(((bf16[512,32,512]{2,1,0:T(8,128)(2,1)}), bf16[512,32,512]{2,1,0:T(8,128)(2,1)}, u32[]{:S(2)}, u32[]{:S(2)}) %all-to-all-start) | async-done | bytes 16777248 | tf_op jit(solution)/shard_map/all_to_all | solution.py:100
  339.5 14.1 %copy.15 = bf16[64,8,32,512]{3,2,1,0:T(8,128)(2,1)} copy(bf16[64,8,32,512]{3,2,0,1:T(8,128)(2,1)} %bitcast.11) | data formatting | bytes 33554432 | tf_op jit(solution)/shard_map/all_to_all | solution.py:100
  353.6 23.7 %reshape.151 = bf16[64,256,1,2,256]{4,3,1,0,2:T(2,128)(2,1)} reshape(bf16[64,8,32,512]{3,2,1,0:T(8,128)(2,1)} %copy.15) | data formatting | bytes 33554432 | tf_op jit(solution)/shard_map/reshape | solution.py:36
  377.3 32.4 %fusion.45 = (bf16[64,256,1,1,256]{4,3,1,0,2:T(2,128)(2,1)}, bf16[64,256,1,1,256]{4,3,1,0,2:T(2,128)(2,1)}) fusion(bf16[64,256,1,2,256]{4,3,1,0,2:T(2,128)(2,1)} %reshape.151), kind=kLoop, calls=%fused_computation.63 | loop fusion | bytes 33554432 | tf_op jit(solution)/shard_map/slice | solution.py:39
  409.7 8.9 %copy.26 = bf16[64,256,1,1,256]{4,1,0,3,2:T(8,128)(2,1)S(1)} copy(bf16[64,256,1,1,256]{4,3,1,0,2:T(2,128)(2,1)} %get-tuple-element.7) | data formatting | bytes 16777216
  418.6 11.9 %copy.27 = bf16[64,256,1,1,256]{4,1,0,3,2:T(8,128)(2,1)S(1)} copy(bf16[64,256,1,1,256]{4,3,1,0,2:T(2,128)(2,1)} %get-tuple-element.8) | data formatting | bytes 16777216
  433.8 3.3 fusion.21
  437.1 9.5 %fusion.17 = f32[64,128,256]{2,1,0:T(8,128)} fusion(bf16[64,256,256]{2,1,0:T(8,128)(2,1)} %bitcast.62, bf16[64,256,256]{2,1,0:T(8,128)(2,1)S(1)} %bitcast.58), kind=kOutput, calls=%fused_computation.29 | convolution fusion | flops 1073741824 | bytes 20971520 | tf_op jit(solution)/shard_map/cik,cjk->cij/dot_general | solution.py:58
  446.6 6.8 fusion.37
  453.4 10.1 %fusion.13 = f32[64,128,128]{2,1,0:T(8,128)} fusion(bf16[64,256,512]{2,1,0:T(8,128)(2,1)} %bitcast.55), kind=kOutput, calls=%fused_computation.21 | convolution fusion | flops 1073741824 | bytes 12582912 | tf_op jit(solution)/shard_map/cik,cjk->cij/dot_general | solution.py:46
  463.5 15.0 %pad_select_fusion = f32[64,128,256]{2,1,0:T(8,128)} fusion(f32[64,128,128]{2,1,0:T(8,128)} %fusion.37, pred[128,256]{1,0:T(8,128)(4,1)S(1)} %iota_compare_fusion.1, bf16[64,256,512]{2,1,0:T(8,128)(2,1)} %bitcast.56), kind=kOutput, calls=%fused_computation.28 | convolution fusion | flops 2149580800 | bytes 37781504 | tf_op jit(solution)/shard_map/cik,cjk->cij/dot_general | solution.py:46
  478.5 14.2 %subtract_select_fusion = f32[64,128,256]{2,1,0:T(8,128)} fusion(f32[64,128,256]{2,1,0:T(8,128)} %fusion.17, f32[64,128,128]{2,1,0:T(8,128)} %fusion.13, pred[128,256]{1,0:T(8,128)(4,1)S(1)} %iota_compare_fusion, bf16[64,256,256]{2,1,0:T(8,128)(2,1)} %bitcast.60, bf16[64,256,256]{2,1,0:T(8,128)(2,1)} %bitcast.64), kind=kOutput, calls=%fused_computation.27 | convolution fusion | flops 1077936128 | bytes 33587200 | tf_op jit(solution)/shard_map/cik,cjk->cij/dot_general | solution.py:52
  492.8 11.4 %maximum_multiply_fusion = f32[64,256,256]{2,1,0:T(8,128)} fusion(f32[64,128,256]{2,1,0:T(8,128)} %subtract_select_fusion, f32[64,128,256]{2,1,0:T(8,128)} %pad_select_fusion), kind=kLoop, calls=%fused_computation.12 | loop fusion | flops 8388608 | bytes 33554432 | tf_op jit(solution)/shard_map/div | solution.py:68
  504.9 279.7 %reduce-scatter.2.cloned.1.call-done = f32[16,256,256]{2,1,0:T(8,128)} async-done(((f32[64,256,256]{2,1,0:T(8,128)}), f32[16,256,256]{2,1,0:T(8,128)}) %reduce-scatter.2.cloned.1.call-update) | async-done | bytes 4194320 | tf_op jit(solution)/shard_map/reduce_scatter | solution.py:101
  784.6 4.7 broadcast_multiply_fusion
  (21 shorter events, 4.5 us)
Async XLA Ops:
  6.5 27.6 %copy-start.3 = (f32[32]{0:T(128)S(1)}, f32[32]{0:T(128)}, u32[]{:S(2)}) copy-start(f32[32]{0:T(128)} %param.6) | copy-start | bytes 388
  6.5 27.9 %copy-start.2 = (f32[4,1024]{1,0:T(4,128)S(1)}, f32[4,1024]{1,0:T(4,128)}, u32[]{:S(2)}) copy-start(f32[4,1024]{1,0:T(4,128)} %param.5) | copy-start | bytes 49156
  22.1 12.4 %collective-permute-start = (bf16[32,3,1024]{2,1,0:T(4,128)(2,1)S(1)}, bf16[32,3,1024]{2,1,0:T(4,128)(2,1)S(1)}, u32[]{:S(2)}, u32[]{:S(2)}) collective-permute-start(bf16[32,3,1024]{2,1,0:T(4,128)(2,1)S(1)} %slice.79), channel_id=1, source_target_pairs={{0,1},{1,2},{2,3},{4,5},{5,6},{6,7},{8,9},{9,10},{10,11},{12,13},{... | collective-permute-start | bytes 589832 | tf_op jit(solution)/shard_map/ppermute | solution.py:12
  150.8 188.7 %all-to-all-start = ((bf16[512,32,512]{2,1,0:T(8,128)(2,1)}), bf16[512,32,512]{2,1,0:T(8,128)(2,1)}, u32[]{:S(2)}, u32[]{:S(2)}) async-start(bf16[512,32,512]{2,1,0:T(8,128)(2,1)} %copy.14), calls=%async_computation | async-start | bytes 33554432 | tf_op jit(solution)/shard_map/all_to_all | solution.py:100
  156.9 627.7 %reduce-scatter.2.cloned.1.call-start = ((), (), s32[]{:S(2)}) async-start(), calls=%async_computation.2 | async-start | bytes 20971520 | tf_op jit(solution)/shard_map/reduce_scatter | solution.py:101
  418.6 28.0 %copy-start = (bf16[64,256,1,1,256]{4,1,0,3,2:T(8,128)(2,1)}, bf16[64,256,1,1,256]{4,1,0,3,2:T(8,128)(2,1)S(1)}, u32[]{:S(2)}) copy-start(bf16[64,256,1,1,256]{4,1,0,3,2:T(8,128)(2,1)S(1)} %copy.26) | copy-start | bytes 25165828
  430.6 3.2 copy-start.1
  504.2 0.7 copy-start.4
Sparse Core Ops, SparseCore 0:
  504.3 280.2 reduce-scatter.1
where the time goes:
time: 799 us; the launch traced here: 796 us
  waiting for transfers between devices  462 us (58%)
  local copies, waits for them, and re-layouts  139 us (17%)
  matrix products  116 us (15%)
  other arithmetic  55.9 us (7%)
  between operations  13.5 us (2%)
  starting transfers between devices  9.63 us (1%)
    reduce_scatter x1, waiting for transfers between devices, on_device(): lax.psum_scatter(gram_blocks(turned, local_frame_count, frame_total), 'tm...  280 us
    all_to_all x1, waiting for transfers between devices, on_device(): lax.all_to_all(spectra, 'feed', split_axis=0, concat_axis=1, tiled=True)  182 us
    dot_general x1, matrix products, on_device(): jnp.einsum('cpn,isn->cips', dft_table, filtered, preferred_element_type=j...  56.9 us
    unnamed x13, local copies, waits for them, and re-layouts  40.1 us
    slice x1, local copies, waits for them, and re-layouts, gram_blocks(): real_half = split[:, :, :, 0].reshape(count_here, inputs_all, columns // 2)  32.4 us
    concatenate x1, local copies, waits for them, and re-layouts, on_device(): jnp.concatenate([real_part, imag_part], axis=2).astype(jnp.bfloat16)  28.6 us
    dot_general x2, matrix products, gram_blocks(): jnp.einsum('cik,cjk->cij', turned[:, first:last], turned[:, first:], pref...  25.1 us
    reshape x1, local copies, waits for them, and re-layouts, gram_blocks(): turned.reshape(count_here, inputs_all, columns // (2 * local_frame_count)...  23.7 us
  transfers between devices with their start and end apart: 3, of which 2 were waited for; matrix products, arithmetic and copies ran while one was open for 1% of the time, Pallas kernels for 0%

commit v1 on v0

v1 whole, which is shorter than its diff:
```python
import functools
import math

import jax
import jax.numpy as jnp
import numpy as np
from jax import lax
from jax.experimental import pallas as pl
from jax.experimental.pallas import tpu as pltpu
from jax.sharding import PartitionSpec as P

VMEM_LIMIT = 56 * 1024 * 1024
SEND_PEAK = 16384.0


def passed_along(block, axis, distance):
    devices = range(lax.axis_size(axis))
    route = [(i - distance, i) for i in devices if i - distance in devices]
    return lax.ppermute(block, axis, route)


def table_rows(channels, fft_length):
    samples = np.arange(fft_length, dtype=np.int64)
    product = channels[:, None].astype(np.int64) * samples[None, :] % fft_length
    angles = product.astype(np.float32) * np.float32(2.0 * math.pi / fft_length)
    rows = np.concatenate([np.cos(angles), -np.sin(angles)], axis=0)
    return rows.astype(jnp.bfloat16)


def dft_kernel(table_ref, cos_ref, sin_ref, filtered_ref, out_ref, *turned):
    inputs, frames = filtered_ref.shape[0], filtered_ref.shape[1]
    rows = table_ref.shape[0] // 2
    width = 128
    for i in range(inputs):
        raw = lax.dot_general(
            table_ref[...], filtered_ref[i], (((1,), (1,)), ((), ())),
            preferred_element_type=jnp.float32,
        )
        real, imag = raw[:rows], raw[rows:]
        cosine = cos_ref[0, :, i : i + 1]
        sine = sin_ref[0, :, i : i + 1]
        both = (real * cosine + imag * sine, imag * cosine - real * sine)
        for q in range(2):
            for piece in range(frames // width):
                turned[q * (frames // width) + piece][pl.ds(i, rows, stride=inputs), :] = both[q][
                    :, piece * width : (piece + 1) * width
                ]
    for piece, ref in enumerate(turned):
        value = ref[...].reshape(rows, inputs, width).astype(jnp.bfloat16)
        out_ref[:, :, piece * width : (piece + 1) * width] = value


def dft_call(table, cosine, sine, filtered):
    blocks, rows, inputs = cosine.shape
    inputs_here, frames, fft_length = filtered.shape
    out_shape = jax.ShapeDtypeStruct((rows, inputs_here, 2 * frames), jnp.bfloat16)
    return pl.pallas_call(
        dft_kernel,
        out_shape=out_shape,
        grid=(blocks,),
        in_specs=[
            pl.BlockSpec((2 * rows, fft_length), lambda b: (0, 0)),
            pl.BlockSpec((1, rows, inputs), lambda b: (b, 0, 0)),
            pl.BlockSpec((1, rows, inputs), lambda b: (b, 0, 0)),
            pl.BlockSpec((inputs, frames, fft_length), lambda b: (b, 0, 0)),
        ],
        out_specs=pl.BlockSpec((rows, inputs, 2 * frames), lambda b: (0, b, 0)),
        scratch_shapes=[pltpu.VMEM((rows * inputs, 128), jnp.float32)] * (2 * frames // 128),
        compiler_params=pltpu.CompilerParams(vmem_limit_bytes=VMEM_LIMIT),
        cost_estimate=pl.CostEstimate(
            flops=4 * rows * inputs_here * frames * fft_length,
            bytes_accessed=2 * inputs_here * frames * (fft_length + 2 * rows),
            transcendentals=0,
        ),
    )(table, cosine, sine, filtered)


def gram_kernel(frame_total, spectra_ref, vis_ref, peak_ref):
    sources, channels, inputs_here, columns = spectra_ref.shape
    total = sources * inputs_here
    half = columns // 2
    row = lax.broadcasted_iota(jnp.int32, (total, total), 0)
    column = lax.broadcasted_iota(jnp.int32, (total, total), 1)
    dims = (((1,), (1,)), ((), ()))
    for c in range(channels):
        slab = spectra_ref[:, c]
        if inputs_here % 16:
            slab = slab.astype(jnp.float32).reshape(total, columns).astype(jnp.bfloat16)
        else:
            slab = slab.reshape(total, columns)
        swapped = jnp.concatenate([slab[:, half:], -slab[:, :half]], axis=1)
        real = lax.dot_general(slab, slab, dims, preferred_element_type=jnp.float32)
        imag = lax.dot_general(swapped, slab, dims, preferred_element_type=jnp.float32)
        packed = jnp.where(row <= column, real, imag)
        peak = jnp.max(jnp.where(row == column, real, 0.0), axis=(0, 1), keepdims=True)
        peak = jnp.maximum(peak, 1e-30)
        vis_ref[c] = (packed * (SEND_PEAK / peak)).astype(vis_ref.dtype)
        peak_ref[c] = jnp.broadcast_to(peak * (1.0 / (SEND_PEAK * frame_total)), (8, 128))


def gram_call(spectra, frame_total):
    sources, channels, inputs_here, columns = spectra.shape
    total = sources * inputs_here
    step = 2 if channels % 2 == 0 else 1
    return pl.pallas_call(
        functools.partial(gram_kernel, frame_total),
        out_shape=(
            jax.ShapeDtypeStruct((channels, total, total), jnp.float32),
            jax.ShapeDtypeStruct((channels, 8, 128), jnp.float32),
        ),
        grid=(channels // step,),
        in_specs=[pl.BlockSpec((sources, step, inputs_here, columns), lambda b: (0, b, 0, 0))],
        out_specs=(
            pl.BlockSpec((step, total, total), lambda b: (b, 0, 0)),
            pl.BlockSpec((step, 8, 128), lambda b: (b, 0, 0)),
        ),
        compiler_params=pltpu.CompilerParams(vmem_limit_bytes=VMEM_LIMIT),
        cost_estimate=pl.CostEstimate(
            flops=4 * channels * total * total * columns,
            bytes_accessed=2 * channels * total * (columns + total),
            transcendentals=0,
        ),
    )(spectra)


def filter_frames(voltages, filter_taps):
    inputs_here, sample_count = voltages.shape
    tap_count, fft_length = filter_taps.shape
    local_frame_count = sample_count // fft_length
    frames = voltages.reshape(inputs_here, local_frame_count, fft_length)
    tail = voltages[:, sample_count - (tap_count - 1) * fft_length :]
    history = passed_along(tail, "tm", 1).reshape(inputs_here, tap_count - 1, fft_length)
    extended = jnp.concatenate([history, frames], axis=1).astype(jnp.float32)
    filtered = filter_taps[0] * extended[:, tap_count - 1 : tap_count - 1 + local_frame_count]
    for tap_index in range(1, tap_count):
        offset = tap_count - 1 - tap_index
        filtered = (
            filtered + filter_taps[tap_index] * extended[:, offset : offset + local_frame_count]
        )
    return filtered.astype(jnp.bfloat16)


def on_device(voltages, filter_taps, delays, channel_flags):
    inputs_here = voltages.shape[0]
    fft_length = filter_taps.shape[1]
    feeds, times = lax.axis_size("feed"), lax.axis_size("tm")
    filtered = filter_frames(voltages, filter_taps)
    frame_total = filtered.shape[1] * times
    owned = channel_flags.shape[0]
    kept = owned // times
    chunks = 4 if kept % 4 == 0 else 1
    width = kept // chunks
    block = 16 if inputs_here % 16 == 0 else inputs_here

    local_flags = lax.dynamic_slice_in_dim(
        channel_flags, lax.axis_index("tm") * kept, kept, 0
    ).astype(jnp.float32)
    scale = 1.0 / math.sqrt(fft_length)
    order = np.arange(feeds * owned).reshape(feeds, times, chunks, width)
    results = []
    for k in range(chunks):
        channels = order[:, :, k].reshape(-1)
        table = jnp.asarray(table_rows(channels, fft_length))
        angles = 2.0 * math.pi / fft_length * jnp.asarray(channels, jnp.float32)[None, :, None]
        angles = angles * delays.reshape(-1, 1, block)
        spectra = dft_call(table, jnp.cos(angles) * scale, jnp.sin(angles) * scale, filtered)
        spectra = spectra.reshape(feeds, times * width, inputs_here, spectra.shape[2])
        turned = lax.all_to_all(spectra, "feed", split_axis=0, concat_axis=0, tiled=True)
        vis, peak = gram_call(turned, frame_total)
        vis = vis.astype(jnp.float16).reshape(times, width, vis.shape[1], vis.shape[2])
        vis = lax.all_to_all(vis, "tm", split_axis=0, concat_axis=0, tiled=True)
        peak = lax.all_gather(peak[:, 0, 0], "tm", axis=0)
        peak = lax.dynamic_slice_in_dim(peak, lax.axis_index("tm") * width, width, 1)
        flags = local_flags[k * width : (k + 1) * width]
        total = jnp.sum(vis.astype(jnp.float32) * peak[:, :, None, None], axis=0)
        results.append(total * flags[:, None, None])
    return jnp.concatenate(results, axis=0)


def solution(mesh):
    in_specs = (P("feed", "tm"), P(), P("feed"), P("feed"))
    out_specs = P(("feed", "tm"), None, None)
    return jax.shard_map(
        on_device, mesh=mesh, in_specs=in_specs, out_specs=out_specs, check_vma=False
    )
```

time: 799 us -> 547 us (0.68)
  waiting for transfers between devices: 462 us -> 232 us
  matrix products: 116 us -> 0 us
  local copies, waits for them, and re-layouts: 139 us -> 26.4 us
  Pallas kernels: 0 us -> 91.1 us
  starting transfers between devices: 9.63 us -> 53.9 us
  blocking collectives: 0 us -> 42.1 us
  other arithmetic: 55.9 us -> 97.8 us
  between operations: 13.5 us -> 0.84 us
    reduce_scatter x1 -> x0, waiting for transfers between devices: 280 us -> none  [on_device(): lax.psum_scatter(gram_blocks(turned, local_frame_count, frame_total), 'tm...]
    dot_general x7 -> x0, matrix products: 116 us -> none  [the longest x1 56.9 us: on_device(): jnp.einsum('cpn,isn->cips', dft_table, filtered, preferred_element_type=j...]
    pallas_call x0 -> x8, Pallas kernels: none -> 91.1 us  [the longest x4 55.5 us: dft_call(): pl.pallas_call(dft_kernel, out_shape=out_shape, grid=(blocks,), in_specs=...]
    convert_element_type x2 -> x7, other arithmetic: 12.1 us -> 84.1 us  [the longest x1 49.5 us: filter_frames(): return filtered.astype(jnp.bfloat16)]
    all_to_all x1 -> x8, waiting for transfers between devices: 182 us -> 232 us  [the longest x4 137 us: on_device(): lax.all_to_all(spectra, 'feed', split_axis=0, concat_axis=0, tiled=True)]
    all_to_all x1 -> x8, starting transfers between devices: 6.14 us -> 50.4 us  [the longest x4 27.5 us: on_device(): vis = lax.all_to_all(vis, 'tm', split_axis=0, concat_axis=0, tiled=True)]
    unnamed x0 -> x1, blocking collectives: none -> 42.1 us
    concatenate x1 -> x0, local copies, waits for them, and re-layouts: 28.6 us -> none  [on_device(): jnp.concatenate([real_part, imag_part], axis=2).astype(jnp.bfloat16)]
  transfers between devices with their start and end apart: 3 -> 9, of which waited for: 2 -> 7; matrix products, arithmetic and copies ran while one was open for 1% -> 9% of each run, Pallas kernels for 0% -> 14%
where the time goes in v1:
time: 547 us; the launch traced here: 544 us
  waiting for transfers between devices  232 us (42%)
  other arithmetic  97.8 us (18%)
  Pallas kernels  91.1 us (17%)
  starting transfers between devices  53.9 us (10%)
  blocking collectives  42.1 us (8%)
  local copies, waits for them, and re-layouts  26.4 us (5%)
    all_to_all x4, waiting for transfers between devices, on_device(): lax.all_to_all(spectra, 'feed', split_axis=0, concat_axis=0, tiled=True)  137 us
    all_to_all x4, waiting for transfers between devices, on_device(): vis = lax.all_to_all(vis, 'tm', split_axis=0, concat_axis=0, tiled=True)  95.8 us
    pallas_call x4, Pallas kernels, dft_call(): pl.pallas_call(dft_kernel, out_shape=out_shape, grid=(blocks,), in_specs=...  55.5 us
    convert_element_type x1, other arithmetic, filter_frames(): return filtered.astype(jnp.bfloat16)  49.5 us
    unnamed x1, blocking collectives  42.1 us
    pallas_call x4, Pallas kernels, gram_call(): pl.pallas_call(functools.partial(gram_kernel, frame_total), out_shape=(ja...  35.6 us
    all_to_all x4, starting transfers between devices, on_device(): vis = lax.all_to_all(vis, 'tm', split_axis=0, concat_axis=0, tiled=True)  27.5 us
    all_to_all x4, starting transfers between devices, on_device(): lax.all_to_all(spectra, 'feed', split_axis=0, concat_axis=0, tiled=True)  22.9 us
  transfers between devices with their start and end apart: 9, of which 7 were waited for; matrix products, arithmetic and copies ran while one was open for 9% of the time, Pallas kernels for 14%

profile of v1, /device:TPU:18, one launch (start us, length us, event | category | flops | bytes accessed | tf_op | source)
XLA Modules:
  0.0 544.4 jit_solution(310823747287734864)
XLA Ops:
  4.5 18.7 %copy.17 = bf16[4,8,256,1024]{3,2,1,0:T(8,128)(2,1)} copy(bf16[4,8,256,1024]{3,1,2,0:T(8,128)(2,1)} %bitcast.16) | data formatting | bytes 33554432
  26.7 19.0 %maximum_convert_fusion = f32[32,259,1024]{2,1,0:T(8,128)} fusion(bf16[32,256,1024]{2,1,0:T(8,128)(2,1)} %bitcast.15, bf16[32,3,1024]{2,1,0:T(4,128)(2,1)S(1)} %reshape.55), kind=kLoop, calls=%fused_computation.8 | loop fusion | flops 33947648 | bytes 50921472 | tf_op jit(solution)/shard_map/convert_element_type | solution.py:133
  45.7 49.5 %fusion.1.filtered_ref = bf16[32,256,1024]{2,1,0:T(8,128)(2,1)} fusion(f32[32,259,1024]{2,1,0:T(8,128)} %maximum_convert_fusion, f32[1024]{0:T(1024)S(1)} %bitcast.23, f32[1024]{0:T(1024)S(1)} %bitcast.24, f32[1024]{0:T(1024)S(1)} %bitcast.22, f32[1024]{0:T(1024)S(1)} %bitcast.21), kind=kLoop, calls=%fused_computation.2 | loop fusion | flops 67108864 | bytes 151011328 | tf_op jit(solution)/shard_map/convert_element_type | solution.py:140
  95.2 13.9 %shard_map.118 = bf16[128,32,512]{2,1,0:T(8,128)(2,1)} custom-call(bf16[256,1024]{1,0:T(8,128)(2,1)} %constant.34.clone.table_ref, f32[2,128,16]{2,1,0:T(8,128)} %get-tuple-element.30.cos_ref, f32[2,128,16]{2,1,0:T(8,128)} %get-tuple-element.29.sin_ref, bf16[32,256,1024]{2,1,0:T(8,128)(2,1)} %fusion.1.filtered_ref), custom_call_target="tpu_custom_call" | custom-call | flops 4294967296 | bytes 20971520 | tf_op jit(solution)/shard_map/pallas_call | solution.py:57
  114.1 13.9 %shard_map.120 = bf16[128,32,512]{2,1,0:T(8,128)(2,1)} custom-call(bf16[256,1024]{1,0:T(8,128)(2,1)} %constant.36.clone.table_ref, f32[2,128,16]{2,1,0:T(8,128)} %get-tuple-element.41.cos_ref, f32[2,128,16]{2,1,0:T(8,128)} %get-tuple-element.42.sin_ref, bf16[32,256,1024]{2,1,0:T(8,128)(2,1)} %fusion.1.filtered_ref), custom_call_target="tpu_custom_call" | custom-call | flops 4294967296 | bytes 20971520 | tf_op jit(solution)/shard_map/pallas_call | solution.py:57
  127.9 33.9 %all-to-all-done.spectra_ref = bf16[8,16,32,512]{3,2,1,0:T(8,128)(2,1)} async-done(((bf16[8,16,32,512]{3,2,1,0:T(8,128)(2,1)}), bf16[8,16,32,512]{3,2,1,0:T(8,128)(2,1)}, u32[]{:S(2)}, u32[]{:S(2)}) %all-to-all-start) | async-done | bytes 4194336 | tf_op jit(solution)/shard_map/all_to_all | solution.py:168
  161.8 6.0 %all-to-all-start.2 = ((bf16[8,16,32,512]{3,2,1,0:T(8,128)(2,1)}), bf16[8,16,32,512]{3,2,1,0:T(8,128)(2,1)}, u32[]{:S(2)}, u32[]{:S(2)}) async-start(bf16[8,16,32,512]{3,2,1,0:T(8,128)(2,1)} %bitcast.19), calls=%async_computation.2 | async-start | bytes 8388608 | tf_op jit(solution)/shard_map/all_to_all | solution.py:168
  167.8 13.9 %shard_map.122 = bf16[128,32,512]{2,1,0:T(8,128)(2,1)} custom-call(bf16[256,1024]{1,0:T(8,128)(2,1)} %constant.38.clone.table_ref, f32[2,128,16]{2,1,0:T(8,128)} %get-tuple-element.39.cos_ref, f32[2,128,16]{2,1,0:T(8,128)} %get-tuple-element.40.sin_ref, bf16[32,256,1024]{2,1,0:T(8,128)(2,1)} %fusion.1.filtered_ref), custom_call_target="tpu_custom_call" | custom-call | flops 4294967296 | bytes 20971520 | tf_op jit(solution)/shard_map/pallas_call | solution.py:57
  181.7 33.8 %all-to-all-done.2.spectra_ref = bf16[8,16,32,512]{3,2,1,0:T(8,128)(2,1)} async-done(((bf16[8,16,32,512]{3,2,1,0:T(8,128)(2,1)}), bf16[8,16,32,512]{3,2,1,0:T(8,128)(2,1)}, u32[]{:S(2)}, u32[]{:S(2)}) %all-to-all-start.2) | async-done | bytes 4194336 | tf_op jit(solution)/shard_map/all_to_all | solution.py:168
  221.5 13.9 %shard_map.124 = bf16[128,32,512]{2,1,0:T(8,128)(2,1)} custom-call(bf16[256,1024]{1,0:T(8,128)(2,1)} %constant.40.clone.table_ref, f32[2,128,16]{2,1,0:T(8,128)} %get-tuple-element.37.cos_ref, f32[2,128,16]{2,1,0:T(8,128)} %get-tuple-element.38.sin_ref, bf16[32,256,1024]{2,1,0:T(8,128)(2,1)} %fusion.1.filtered_ref), custom_call_target="tpu_custom_call" | custom-call | flops 4294967296 | bytes 20971520 | tf_op jit(solution)/shard_map/pallas_call | solution.py:57
  235.3 33.9 %all-to-all-done.4.spectra_ref = bf16[8,16,32,512]{3,2,1,0:T(8,128)(2,1)} async-done(((bf16[8,16,32,512]{3,2,1,0:T(8,128)(2,1)}), bf16[8,16,32,512]{3,2,1,0:T(8,128)(2,1)}, u32[]{:S(2)}, u32[]{:S(2)}) %all-to-all-start.4) | async-done | bytes 4194336 | tf_op jit(solution)/shard_map/all_to_all | solution.py:168
  269.2 6.0 %all-to-all-start.6 = ((bf16[8,16,32,512]{3,2,1,0:T(8,128)(2,1)}), bf16[8,16,32,512]{3,2,1,0:T(8,128)(2,1)}, u32[]{:S(2)}, u32[]{:S(2)}) async-start(bf16[8,16,32,512]{3,2,1,0:T(8,128)(2,1)} %bitcast.17), calls=%async_computation.6 | async-start | bytes 8388608 | tf_op jit(solution)/shard_map/all_to_all | solution.py:168
  275.2 8.9 %shard_map.119 = (f32[16,256,256]{2,1,0:T(8,128)}, f32[16,8,128]{2,1,0:T(8,128)}) custom-call(bf16[8,16,32,512]{3,2,1,0:T(8,128)(2,1)} %all-to-all-done.spectra_ref), custom_call_target="tpu_custom_call" | custom-call | flops 2147483648 | bytes 6291456 | tf_op jit(solution)/shard_map/pallas_call | solution.py:105
  287.9 34.9 %all-to-all-done.6.spectra_ref = bf16[8,16,32,512]{3,2,1,0:T(8,128)(2,1)} async-done(((bf16[8,16,32,512]{3,2,1,0:T(8,128)(2,1)}), bf16[8,16,32,512]{3,2,1,0:T(8,128)(2,1)}, u32[]{:S(2)}, u32[]{:S(2)}) %all-to-all-start.6) | async-done | bytes 4194336 | tf_op jit(solution)/shard_map/all_to_all | solution.py:168
  327.1 8.9 %shard_map.121 = (f32[16,256,256]{2,1,0:T(8,128)}, f32[16,8,128]{2,1,0:T(8,128)}) custom-call(bf16[8,16,32,512]{3,2,1,0:T(8,128)(2,1)} %all-to-all-done.2.spectra_ref), custom_call_target="tpu_custom_call" | custom-call | flops 2147483648 | bytes 6291456 | tf_op jit(solution)/shard_map/pallas_call | solution.py:105
  339.8 32.4 %all-to-all-done.1 = f16[4,4,256,256]{3,2,1,0:T(8,128)(2,1)S(1)} async-done(((f16[4,4,256,256]{3,2,1,0:T(8,128)(2,1)}), f16[4,4,256,256]{3,2,1,0:T(8,128)(2,1)S(1)}, u32[]{:S(2)}, u32[]{:S(2)}) %all-to-all-start.1) | async-done | bytes 2097184 | tf_op jit(solution)/shard_map/all_to_all | solution.py:171
  372.3 7.7 %all-to-all-start.3 = ((f16[4,4,256,256]{3,2,1,0:T(8,128)(2,1)}), f16[4,4,256,256]{3,2,1,0:T(8,128)(2,1)}, u32[]{:S(2)}, u32[]{:S(2)}) async-start(f16[4,4,256,256]{3,2,1,0:T(8,128)(2,1)} %bitcast.8), calls=%async_computation.3 | async-start | bytes 4194304 | tf_op jit(solution)/shard_map/all_to_all | solution.py:171
  380.0 8.9 %shard_map.123 = (f32[16,256,256]{2,1,0:T(8,128)}, f32[16,8,128]{2,1,0:T(8,128)}) custom-call(bf16[8,16,32,512]{3,2,1,0:T(8,128)(2,1)} %all-to-all-done.4.spectra_ref), custom_call_target="tpu_custom_call" | custom-call | flops 2147483648 | bytes 6291456 | tf_op jit(solution)/shard_map/pallas_call | solution.py:105
  392.7 31.7 %all-to-all-done.3 = f16[4,4,256,256]{3,2,1,0:T(8,128)(2,1)} async-done(((f16[4,4,256,256]{3,2,1,0:T(8,128)(2,1)}), f16[4,4,256,256]{3,2,1,0:T(8,128)(2,1)}, u32[]{:S(2)}, u32[]{:S(2)}) %all-to-all-start.3) | async-done | bytes 2097184 | tf_op jit(solution)/shard_map/all_to_all | solution.py:171
  424.4 7.8 %all-to-all-start.5 = ((f16[4,4,256,256]{3,2,1,0:T(8,128)(2,1)}), f16[4,4,256,256]{3,2,1,0:T(8,128)(2,1)}, u32[]{:S(2)}, u32[]{:S(2)}) async-start(f16[4,4,256,256]{3,2,1,0:T(8,128)(2,1)} %bitcast.10), calls=%async_computation.5 | async-start | bytes 4194304 | tf_op jit(solution)/shard_map/all_to_all | solution.py:171
  432.2 8.9 %shard_map.125 = (f32[16,256,256]{2,1,0:T(8,128)}, f32[16,8,128]{2,1,0:T(8,128)}) custom-call(bf16[8,16,32,512]{3,2,1,0:T(8,128)(2,1)} %all-to-all-done.6.spectra_ref), custom_call_target="tpu_custom_call" | custom-call | flops 2147483648 | bytes 6291456 | tf_op jit(solution)/shard_map/pallas_call | solution.py:105
  445.0 31.6 %all-to-all-done.5 = f16[4,4,256,256]{3,2,1,0:T(8,128)(2,1)} async-done(((f16[4,4,256,256]{3,2,1,0:T(8,128)(2,1)}), f16[4,4,256,256]{3,2,1,0:T(8,128)(2,1)}, u32[]{:S(2)}, u32[]{:S(2)}) %all-to-all-start.5) | async-done | bytes 2097184 | tf_op jit(solution)/shard_map/all_to_all | solution.py:171
  476.6 7.8 %all-to-all-start.7 = ((f16[4,4,256,256]{3,2,1,0:T(8,128)(2,1)}), f16[4,4,256,256]{3,2,1,0:T(8,128)(2,1)}, u32[]{:S(2)}, u32[]{:S(2)}) async-start(f16[4,4,256,256]{3,2,1,0:T(8,128)(2,1)} %bitcast.12), calls=%async_computation.7 | async-start | bytes 4194304 | tf_op jit(solution)/shard_map/all_to_all | solution.py:171
  491.3 42.1 %all-reduce.8 = (f32[4,16]{1,0:T(4,128)S(1)}, f32[4,16]{1,0:T(4,128)S(1)}, f32[4,16]{1,0:T(4,128)S(1)}, f32[4,16]{1,0:T(4,128)S(1)}) all-reduce(f32[4,16]{1,0:T(4,128)S(1)} %reshape.68, f32[4,16]{1,0:T(4,128)S(1)} %reshape.67, f32[4,16]{1,0:T(4,128)S(1)} %reshape.66, f32[4,16]{1,0:T(4,128)S(1)} %reshape.65), channel_id=5, replica_groups=mesh['feed'=8,'tm'=4] {'tm'}, use_global_device_ids=true, to_apply=%add.3 | all-reduce | flops 256 | bytes 2048
  (63 shorter events, 55.7 us)
Async XLA Ops:
  0.9 25.4 %collective-permute-start = (bf16[32,3072]{1,0:T(8,128)(2,1)S(1)}, bf16[32,3072]{1,0:T(8,128)(2,1)S(1)}, u32[]{:S(2)}, u32[]{:S(2)}) collective-permute-start(bf16[32,3072]{1,0:T(8,128)(2,1)S(1)} %slice.52), channel_id=1, source_target_pairs={{0,1},{1,2},{2,3},{4,5},{5,6},{6,7},{8,9},{9,10},{10,11},{12,13},{... | collective-permute-start | bytes 589832 | tf_op jit(solution)/shard_map/ppermute | solution.py:19
  4.4 18.7 %copy-start.5 = (f32[32]{0:T(128)S(1)}, f32[32]{0:T(128)}, u32[]{:S(2)}) copy-start(f32[32]{0:T(128)} %param.14) | copy-start | bytes 388
  4.4 18.8 %copy-start.1 = (f32[128]{0:T(128)S(1)}, f32[128]{0:T(128)}, u32[]{:S(2)}) copy-start(f32[128]{0:T(128)} %constant.42) | copy-start | bytes 1540
  4.5 18.8 %copy-start.2 = (f32[128]{0:T(128)S(1)}, f32[128]{0:T(128)}, u32[]{:S(2)}) copy-start(f32[128]{0:T(128)} %constant.43) | copy-start | bytes 1540
  4.5 18.8 %copy-start.3 = (f32[128]{0:T(128)S(1)}, f32[128]{0:T(128)}, u32[]{:S(2)}) copy-start(f32[128]{0:T(128)} %constant.44) | copy-start | bytes 1540
  4.5 18.8 %copy-start.4 = (f32[128]{0:T(128)S(1)}, f32[128]{0:T(128)}, u32[]{:S(2)}) copy-start(f32[128]{0:T(128)} %constant.45) | copy-start | bytes 1540
  4.5 21.9 %copy-start = (f32[4,1024]{1,0:T(4,128)S(1)}, f32[4,1024]{1,0:T(4,128)}, u32[]{:S(2)}) copy-start(f32[4,1024]{1,0:T(4,128)} %param.13) | copy-start | bytes 49156
  109.1 52.7 %all-to-all-start = ((bf16[8,16,32,512]{3,2,1,0:T(8,128)(2,1)}), bf16[8,16,32,512]{3,2,1,0:T(8,128)(2,1)}, u32[]{:S(2)}, u32[]{:S(2)}) async-start(bf16[8,16,32,512]{3,2,1,0:T(8,128)(2,1)} %bitcast.20), calls=%async_computation | async-start | bytes 8388608 | tf_op jit(solution)/shard_map/all_to_all | solution.py:168
  161.8 53.7 %all-to-all-start.2 = ((bf16[8,16,32,512]{3,2,1,0:T(8,128)(2,1)}), bf16[8,16,32,512]{3,2,1,0:T(8,128)(2,1)}, u32[]{:S(2)}, u32[]{:S(2)}) async-start(bf16[8,16,32,512]{3,2,1,0:T(8,128)(2,1)} %bitcast.19), calls=%async_computation.2 | async-start | bytes 8388608 | tf_op jit(solution)/shard_map/all_to_all | solution.py:168
  215.5 53.7 %all-to-all-start.4 = ((bf16[8,16,32,512]{3,2,1,0:T(8,128)(2,1)}), bf16[8,16,32,512]{3,2,1,0:T(8,128)(2,1)}, u32[]{:S(2)}, u32[]{:S(2)}) async-start(bf16[8,16,32,512]{3,2,1,0:T(8,128)(2,1)} %bitcast.18), calls=%async_computation.4 | async-start | bytes 8388608 | tf_op jit(solution)/shard_map/all_to_all | solution.py:168
  269.2 53.7 %all-to-all-start.6 = ((bf16[8,16,32,512]{3,2,1,0:T(8,128)(2,1)}), bf16[8,16,32,512]{3,2,1,0:T(8,128)(2,1)}, u32[]{:S(2)}, u32[]{:S(2)}) async-start(bf16[8,16,32,512]{3,2,1,0:T(8,128)(2,1)} %bitcast.17), calls=%async_computation.6 | async-start | bytes 8388608 | tf_op jit(solution)/shard_map/all_to_all | solution.py:168
  322.9 49.4 %all-to-all-start.1 = ((f16[4,4,256,256]{3,2,1,0:T(8,128)(2,1)}), f16[4,4,256,256]{3,2,1,0:T(8,128)(2,1)S(1)}, u32[]{:S(2)}, u32[]{:S(2)}) async-start(f16[4,4,256,256]{3,2,1,0:T(8,128)(2,1)} %bitcast.5), calls=%async_computation.1 | async-start | bytes 4194304 | tf_op jit(solution)/shard_map/all_to_all | solution.py:171
  372.3 52.2 %all-to-all-start.3 = ((f16[4,4,256,256]{3,2,1,0:T(8,128)(2,1)}), f16[4,4,256,256]{3,2,1,0:T(8,128)(2,1)}, u32[]{:S(2)}, u32[]{:S(2)}) async-start(f16[4,4,256,256]{3,2,1,0:T(8,128)(2,1)} %bitcast.8), calls=%async_computation.3 | async-start | bytes 4194304 | tf_op jit(solution)/shard_map/all_to_all | solution.py:171
  424.4 52.2 %all-to-all-start.5 = ((f16[4,4,256,256]{3,2,1,0:T(8,128)(2,1)}), f16[4,4,256,256]{3,2,1,0:T(8,128)(2,1)}, u32[]{:S(2)}, u32[]{:S(2)}) async-start(f16[4,4,256,256]{3,2,1,0:T(8,128)(2,1)} %bitcast.10), calls=%async_computation.5 | async-start | bytes 4194304 | tf_op jit(solution)/shard_map/all_to_all | solution.py:171
  441.1 43.3 %copy-start.7 = (u32[32]{0:T(128)S(1)}, u32[32]{0:T(128)}, u32[]{:S(2)}) copy-start(u32[32]{0:T(128)} %constant.48) | copy-start | bytes 388
  441.1 44.5 %copy-start.6 = (s32[64]{0:T(128)S(1)}, s32[64]{0:T(128)}, u32[]{:S(2)}) copy-start(s32[64]{0:T(128)} %param.15) | copy-start | bytes 772
  476.6 62.8 %all-to-all-start.7 = ((f16[4,4,256,256]{3,2,1,0:T(8,128)(2,1)}), f16[4,4,256,256]{3,2,1,0:T(8,128)(2,1)}, u32[]{:S(2)}, u32[]{:S(2)}) async-start(f16[4,4,256,256]{3,2,1,0:T(8,128)(2,1)} %bitcast.12), calls=%async_computation.7 | async-start | bytes 4194304 | tf_op jit(solution)/shard_map/all_to_all | solution.py:171

commit v2 on v1

--- a/solution.py
+++ b/solution.py
@@ -11,6 +11,7 @@
 
 VMEM_LIMIT = 56 * 1024 * 1024
 SEND_PEAK = 16384.0
+EXTRA_ROWS = 8
 
 
 def passed_along(block, axis, distance):
@@ -75,7 +76,7 @@
     )(table, cosine, sine, filtered)
 
 
-def gram_kernel(frame_total, spectra_ref, vis_ref, peak_ref):
+def gram_kernel(spectra_ref, vis_ref):
     sources, channels, inputs_here, columns = spectra_ref.shape
     total = sources * inputs_here
     half = columns // 2
@@ -94,50 +95,89 @@
         packed = jnp.where(row <= column, real, imag)
         peak = jnp.max(jnp.where(row == column, real, 0.0), axis=(0, 1), keepdims=True)
         peak = jnp.maximum(peak, 1e-30)
-        vis_ref[c] = (packed * (SEND_PEAK / peak)).astype(vis_ref.dtype)
-        peak_ref[c] = jnp.broadcast_to(peak * (1.0 / (SEND_PEAK * frame_total)), (8, 128))
-
-
-def gram_call(spectra, frame_total):
+        power = jnp.ceil(jnp.log2(peak))
+        vis_ref[c, :total] = packed * (SEND_PEAK * jnp.exp2(-power))
+        vis_ref[c, total:] = jnp.broadcast_to(power, (EXTRA_ROWS, total))
+
+
+def gram_call(spectra):
     sources, channels, inputs_here, columns = spectra.shape
     total = sources * inputs_here
     step = 2 if channels % 2 == 0 else 1
     return pl.pallas_call(
-        functools.partial(gram_kernel, frame_total),
-        out_shape=(
-            jax.ShapeDtypeStruct((channels, total, total), jnp.float32),
-            jax.ShapeDtypeStruct((channels, 8, 128), jnp.float32),
-        ),
+        gram_kernel,
+        out_shape=jax.ShapeDtypeStruct((channels, total + EXTRA_ROWS, total), jnp.float32),
         grid=(channels // step,),
         in_specs=[pl.BlockSpec((sources, step, inputs_here, columns), lambda b: (0, b, 0, 0))],
-        out_specs=(
-            pl.BlockSpec((step, total, total), lambda b: (b, 0, 0)),
-            pl.BlockSpec((step, 8, 128), lambda b: (b, 0, 0)),
-        ),
+        out_specs=pl.BlockSpec((step, total + EXTRA_ROWS, total), lambda b: (b, 0, 0)),
         compiler_params=pltpu.CompilerParams(vmem_limit_bytes=VMEM_LIMIT),
         cost_estimate=pl.CostEstimate(
             flops=4 * channels * total * total * columns,
-            bytes_accessed=2 * channels * total * (columns + total),
+            bytes_accessed=2 * channels * total * (columns + 2 * total),
             transcendentals=0,
         ),
     )(spectra)
 
 
+def filter_kernel(history_ref, taps_ref, block_ref, out_ref, carry, turned):
+    tap_count, fft_length = taps_ref.shape
+    inputs, group = out_ref.shape[0], out_ref.shape[1]
+    kept = tap_count - 1
+
+    @pl.when(pl.program_id(0) == 0)
+    def _():
+        carry[...] = history_ref[...]
+
+    def piece(p, unused):
+        lanes = pl.multiple_of(p * 128, 128)
+        taps = [taps_ref[t : t + 1, pl.ds(lanes, 128)] for t in range(tap_count)]
+        frames = [
+            carry[:, pl.ds(pl.multiple_of(h * fft_length + lanes, 128), 128)].astype(jnp.float32)
+            for h in range(kept)
+        ]
+        for m in range(group):
+            start = pl.multiple_of(m * fft_length + lanes, 128)
+            frames.append(block_ref[:, pl.ds(start, 128)].astype(jnp.float32))
+            value = taps[0] * frames[-1]
+            for t in range(1, tap_count):
+                value = value + taps[t] * frames[-1 - t]
+            turned[pl.ds(m, inputs, stride=group), :] = value
+        result = turned[...].reshape(inputs, group, 128).astype(jnp.bfloat16)
+        out_ref[:, :, pl.ds(lanes, 128)] = result
+        return unused
+
+    lax.fori_loop(0, fft_length // 128, piece, 0)
+    carry[...] = block_ref[:, (group - kept) * fft_length :]
+
+
 def filter_frames(voltages, filter_taps):
     inputs_here, sample_count = voltages.shape
     tap_count, fft_length = filter_taps.shape
-    local_frame_count = sample_count // fft_length
-    frames = voltages.reshape(inputs_here, local_frame_count, fft_length)
-    tail = voltages[:, sample_count - (tap_count - 1) * fft_length :]
-    history = passed_along(tail, "tm", 1).reshape(inputs_here, tap_count - 1, fft_length)
-    extended = jnp.concatenate([history, frames], axis=1).astype(jnp.float32)
-    filtered = filter_taps[0] * extended[:, tap_count - 1 : tap_count - 1 + local_frame_count]
-    for tap_index in range(1, tap_count):
-        offset = tap_count - 1 - tap_index
-        filtered = (
-            filtered + filter_taps[tap_index] * extended[:, offset : offset + local_frame_count]
-        )
-    return filtered.astype(jnp.bfloat16)
+    frames = sample_count // fft_length
+    kept = (tap_count - 1) * fft_length
+    group = 16
+    history = passed_along(voltages[:, sample_count - kept :], "tm", 1)
+    return pl.pallas_call(
+        filter_kernel,
+        out_shape=jax.ShapeDtypeStruct((inputs_here, frames, fft_length), jnp.bfloat16),
+        grid=(frames // group,),
+        in_specs=[
+            pl.BlockSpec((inputs_here, kept), lambda b: (0, 0)),
+            pl.BlockSpec((tap_count, fft_length), lambda b: (0, 0)),
+            pl.BlockSpec((inputs_here, group * fft_length), lambda b: (0, b)),
+        ],
+        out_specs=pl.BlockSpec((inputs_here, group, fft_length), lambda b: (0, b, 0)),
+        scratch_shapes=[
+            pltpu.VMEM((inputs_here, kept), jnp.bfloat16),
+            pltpu.VMEM((inputs_here * group, 128), jnp.float32),
+        ],
+        compiler_params=pltpu.CompilerParams(vmem_limit_bytes=VMEM_LIMIT),
+        cost_estimate=pl.CostEstimate(
+            flops=8 * inputs_here * sample_count,
+            bytes_accessed=4 * inputs_here * sample_count,
+            transcendentals=0,
+        ),
+    )(history, filter_taps, voltages)
 
 
 def on_device(voltages, filter_taps, delays, channel_flags):
@@ -157,22 +197,33 @@
     ).astype(jnp.float32)
     scale = 1.0 / math.sqrt(fft_length)
     order = np.arange(feeds * owned).reshape(feeds, times, chunks, width)
+    place = lax.axis_index("tm")
     results = []
+    sent = []
     for k in range(chunks):
         channels = order[:, :, k].reshape(-1)
         table = jnp.asarray(table_rows(channels, fft_length))
         angles = 2.0 * math.pi / fft_length * jnp.asarray(channels, jnp.float32)[None, :, None]
         angles = angles * delays.reshape(-1, 1, block)
+        if k >= 2:
+            filtered, sent[k - 2] = lax.optimization_barrier((filtered, sent[k - 2]))
         spectra = dft_call(table, jnp.cos(angles) * scale, jnp.sin(angles) * scale, filtered)
         spectra = spectra.reshape(feeds, times * width, inputs_here, spectra.shape[2])
         turned = lax.all_to_all(spectra, "feed", split_axis=0, concat_axis=0, tiled=True)
-        vis, peak = gram_call(turned, frame_total)
-        vis = vis.astype(jnp.float16).reshape(times, width, vis.shape[1], vis.shape[2])
-        vis = lax.all_to_all(vis, "tm", split_axis=0, concat_axis=0, tiled=True)
-        peak = lax.all_gather(peak[:, 0, 0], "tm", axis=0)
-        peak = lax.dynamic_slice_in_dim(peak, lax.axis_index("tm") * width, width, 1)
-        flags = local_flags[k * width : (k + 1) * width]
-        total = jnp.sum(vis.astype(jnp.float32) * peak[:, :, None, None], axis=0)
+        vis = gram_call(turned).astype(jnp.float16)
+        sent.append(vis.reshape(times, width, vis.shape[1], vis.shape[2]))
+    for k in range(chunks):
+        flags = local_flags[k * width : (k + 1) * width] * (1.0 / (SEND_PEAK * frame_total))
+        total = 0.0
+        for shift in range(times):
+            target = lax.rem(place + shift, times)
+            part = lax.dynamic_index_in_dim(sent[k], target, 0, keepdims=False)
+            if shift:
+                route = [(i, (i + shift) % times) for i in range(times)]
+                part = lax.ppermute(part, "tm", route)
+            part = part.astype(jnp.float32)
+            count = part.shape[2]
+            total = total + part[:, :count] * jnp.exp2(part[:, count:, :1][:, :1])
         results.append(total * flags[:, None, None])
     return jnp.concatenate(results, axis=0)
 

time: 547 us -> 433 us (0.79)
  other arithmetic: 97.8 us -> 32.8 us
  blocking collectives: 42.1 us -> 0 us
  Pallas kernels: 91.1 us -> 118 us
  local copies, waits for them, and re-layouts: 26.4 us -> 4.04 us
  starting transfers between devices: 53.9 us -> 42.3 us
    ppermute x0 -> x12, waiting for transfers between devices: none -> 154 us  [on_device(): part = lax.ppermute(part, 'tm', route)]
    all_to_all x4 -> x0, waiting for transfers between devices: 95.8 us -> none  [on_device(): vis = lax.all_to_all(vis, 'tm', split_axis=0, concat_axis=0, tiled=True)]
    convert_element_type x6 -> x20, other arithmetic: 84 us -> 22 us  [the longest x4 11.4 us: on_device(): vis = gram_call(turned).astype(jnp.float16)]
    all_to_all x4, waiting for transfers between devices: 137 us -> 77.2 us  [on_device(): lax.all_to_all(spectra, 'feed', split_axis=0, concat_axis=0, tiled=True)]
    unnamed x1 -> x0, blocking collectives: 42.1 us -> none
    all_to_all x4 -> x0, starting transfers between devices: 27.5 us -> none  [on_device(): vis = lax.all_to_all(vis, 'tm', split_axis=0, concat_axis=0, tiled=True)]
    pallas_call x4 -> x5, Pallas kernels: 35.6 us -> 62.2 us  [the longest x4 35.8 us: gram_call(): pl.pallas_call(gram_kernel, out_shape=jax.ShapeDtypeStruct((channels, tot...]
    unnamed x26 -> x16, local copies, waits for them, and re-layouts: 20.2 us -> 2.36 us
  transfers between devices with their start and end apart: 9 -> 17, of which waited for: 7 -> 12; matrix products, arithmetic and copies ran while one was open for 9% -> 7% of each run, Pallas kernels for 14% -> 18%
where the time goes in v2:
time: 433 us; the launch traced here: 429 us
  waiting for transfers between devices  232 us (54%)
  Pallas kernels  118 us (27%)
  starting transfers between devices  42.3 us (10%)
  other arithmetic  32.8 us (8%)
    ppermute x12, waiting for transfers between devices, on_device(): part = lax.ppermute(part, 'tm', route)  154 us
    all_to_all x4, waiting for transfers between devices, on_device(): lax.all_to_all(spectra, 'feed', split_axis=0, concat_axis=0, tiled=True)  77.2 us
    pallas_call x4, Pallas kernels, dft_call(): pl.pallas_call(dft_kernel, out_shape=out_shape, grid=(blocks,), in_specs=...  55.6 us
    pallas_call x4, Pallas kernels, gram_call(): pl.pallas_call(gram_kernel, out_shape=jax.ShapeDtypeStruct((channels, tot...  35.8 us
    pallas_call x1, Pallas kernels, filter_frames(): pl.pallas_call(filter_kernel, out_shape=jax.ShapeDtypeStruct((inputs_here...  26.4 us
    all_to_all x4, starting transfers between devices, on_device(): lax.all_to_all(spectra, 'feed', split_axis=0, concat_axis=0, tiled=True)  22.9 us
    ppermute x12, starting transfers between devices, on_device(): part = lax.ppermute(part, 'tm', route)  15.9 us
    convert_element_type x4, other arithmetic, on_device(): vis = gram_call(turned).astype(jnp.float16)  11.4 us
  transfers between devices with their start and end apart: 17, of which 12 were waited for; matrix products, arithmetic and copies ran while one was open for 7% of the time, Pallas kernels for 18%

profile of v2, /device:TPU:18, one launch (start us, length us, event | category | flops | bytes accessed | tf_op | source)
XLA Modules:
  0.0 428.8 jit_solution(2624110988325484378)
XLA Ops:
  10.2 26.4 %shard_map.118.filtered_ref = bf16[32,256,1024]{2,1,0:T(8,128)(2,1)} custom-call(bf16[32,3072]{1,0:T(8,128)(2,1)} %copy-done.6, f32[4,1024]{1,0:T(4,128)} %taps_ref.1, bf16[32,262144]{1,0:T(8,128)(2,1)} %block_ref.1), custom_call_target="tpu_custom_call" | custom-call | flops 67108864 | bytes 33554432 | tf_op jit(solution)/shard_map/pallas_call | solution.py:160
  36.5 13.9 %shard_map.119 = bf16[128,32,512]{2,1,0:T(8,128)(2,1)} custom-call(bf16[256,1024]{1,0:T(8,128)(2,1)} %constant.84.clone.table_ref, f32[2,128,16]{2,1,0:T(8,128)} %get-tuple-element.41.cos_ref, f32[2,128,16]{2,1,0:T(8,128)} %get-tuple-element.42.sin_ref, bf16[32,256,1024]{2,1,0:T(8,128)(2,1)} %shard_map.118.filtered_ref), custom_call_target="tpu_custom_call" | custom-call | flops 4294967296 | bytes 20971520 | tf_op jit(solution)/shard_map/pallas_call | solution.py:58
  50.4 5.0 %all-to-all-start = ((bf16[8,16,32,512]{3,2,1,0:T(8,128)(2,1)}), bf16[8,16,32,512]{3,2,1,0:T(8,128)(2,1)}, u32[]{:S(2)}, u32[]{:S(2)}) async-start(bf16[8,16,32,512]{3,2,1,0:T(8,128)(2,1)} %bitcast.47), calls=%async_computation | async-start | bytes 8388608 | tf_op jit(solution)/shard_map/all_to_all | solution.py:212
  55.4 13.9 %shard_map.121 = bf16[128,32,512]{2,1,0:T(8,128)(2,1)} custom-call(bf16[256,1024]{1,0:T(8,128)(2,1)} %constant.86.clone.table_ref, f32[2,128,16]{2,1,0:T(8,128)} %get-tuple-element.39.cos_ref, f32[2,128,16]{2,1,0:T(8,128)} %get-tuple-element.40.sin_ref, bf16[32,256,1024]{2,1,0:T(8,128)(2,1)} %shard_map.118.filtered_ref), custom_call_target="tpu_custom_call" | custom-call | flops 4294967296 | bytes 20971520 | tf_op jit(solution)/shard_map/pallas_call | solution.py:58
  69.3 33.9 %all-to-all-done.spectra_ref = bf16[8,16,32,512]{3,2,1,0:T(8,128)(2,1)} async-done(((bf16[8,16,32,512]{3,2,1,0:T(8,128)(2,1)}), bf16[8,16,32,512]{3,2,1,0:T(8,128)(2,1)}, u32[]{:S(2)}, u32[]{:S(2)}) %all-to-all-start) | async-done | bytes 4194336 | tf_op jit(solution)/shard_map/all_to_all | solution.py:212
  103.1 6.0 %all-to-all-start.1 = ((bf16[8,16,32,512]{3,2,1,0:T(8,128)(2,1)}), bf16[8,16,32,512]{3,2,1,0:T(8,128)(2,1)}, u32[]{:S(2)}, u32[]{:S(2)}) async-start(bf16[8,16,32,512]{3,2,1,0:T(8,128)(2,1)} %bitcast.46), calls=%async_computation.1 | async-start | bytes 8388608 | tf_op jit(solution)/shard_map/all_to_all | solution.py:212
  109.1 9.0 %shard_map.120 = f32[16,264,256]{2,1,0:T(8,128)} custom-call(bf16[8,16,32,512]{3,2,1,0:T(8,128)(2,1)} %all-to-all-done.spectra_ref), custom_call_target="tpu_custom_call" | custom-call | flops 2147483648 | bytes 8388608 | tf_op jit(solution)/shard_map/pallas_call | solution.py:107
  121.9 13.9 %shard_map.123 = bf16[128,32,512]{2,1,0:T(8,128)(2,1)} custom-call(bf16[256,1024]{1,0:T(8,128)(2,1)} %constant.88.clone.table_ref, f32[2,128,16]{2,1,0:T(8,128)} %get-tuple-element.30.cos_ref, f32[2,128,16]{2,1,0:T(8,128)} %get-tuple-element.29.sin_ref, bf16[32,256,1024]{2,1,0:T(8,128)(2,1)} %shard_map.118.filtered_ref), custom_call_target="tpu_custom_call" | custom-call | flops 4294967296 | bytes 20971520 | tf_op jit(solution)/shard_map/pallas_call | solution.py:58
  135.9 21.0 %all-to-all-done.1.spectra_ref = bf16[8,16,32,512]{3,2,1,0:T(8,128)(2,1)} async-done(((bf16[8,16,32,512]{3,2,1,0:T(8,128)(2,1)}), bf16[8,16,32,512]{3,2,1,0:T(8,128)(2,1)}, u32[]{:S(2)}, u32[]{:S(2)}) %all-to-all-start.1) | async-done | bytes 4194336 | tf_op jit(solution)/shard_map/all_to_all | solution.py:212
  156.9 6.0 %all-to-all-start.2 = ((bf16[8,16,32,512]{3,2,1,0:T(8,128)(2,1)}), bf16[8,16,32,512]{3,2,1,0:T(8,128)(2,1)}, u32[]{:S(2)}, u32[]{:S(2)}) async-start(bf16[8,16,32,512]{3,2,1,0:T(8,128)(2,1)} %bitcast.45), calls=%async_computation.2 | async-start | bytes 8388608 | tf_op jit(solution)/shard_map/all_to_all | solution.py:212
  162.8 9.0 %shard_map.122 = f32[16,264,256]{2,1,0:T(8,128)} custom-call(bf16[8,16,32,512]{3,2,1,0:T(8,128)(2,1)} %all-to-all-done.1.spectra_ref), custom_call_target="tpu_custom_call" | custom-call | flops 2147483648 | bytes 8388608 | tf_op jit(solution)/shard_map/pallas_call | solution.py:107
  174.3 13.9 %shard_map.125 = bf16[128,32,512]{2,1,0:T(8,128)(2,1)} custom-call(bf16[256,1024]{1,0:T(8,128)(2,1)} %constant.90.clone.table_ref, f32[2,128,16]{2,1,0:T(8,128)} %get-tuple-element.37.cos_ref, f32[2,128,16]{2,1,0:T(8,128)} %get-tuple-element.38.sin_ref, bf16[32,256,1024]{2,1,0:T(8,128)(2,1)} %shard_map.118.filtered_ref), custom_call_target="tpu_custom_call" | custom-call | flops 4294967296 | bytes 20971520 | tf_op jit(solution)/shard_map/pallas_call | solution.py:58
  188.2 22.4 %all-to-all-done.2.spectra_ref = bf16[8,16,32,512]{3,2,1,0:T(8,128)(2,1)} async-done(((bf16[8,16,32,512]{3,2,1,0:T(8,128)(2,1)}), bf16[8,16,32,512]{3,2,1,0:T(8,128)(2,1)}, u32[]{:S(2)}, u32[]{:S(2)}) %all-to-all-start.2) | async-done | bytes 4194336 | tf_op jit(solution)/shard_map/all_to_all | solution.py:212
  210.6 6.0 %all-to-all-start.3 = ((bf16[8,16,32,512]{3,2,1,0:T(8,128)(2,1)}), bf16[8,16,32,512]{3,2,1,0:T(8,128)(2,1)}, u32[]{:S(2)}, u32[]{:S(2)}) async-start(bf16[8,16,32,512]{3,2,1,0:T(8,128)(2,1)} %bitcast.44), calls=%async_computation.3 | async-start | bytes 8388608 | tf_op jit(solution)/shard_map/all_to_all | solution.py:212
  226.4 31.7 %collective-permute-done.1 = f16[4,264,256]{2,1,0:T(8,128)(2,1)} collective-permute-done((f16[4,264,256]{2,1,0:T(8,128)(2,1)}, f16[4,264,256]{2,1,0:T(8,128)(2,1)}, u32[]{:S(2)}, u32[]{:S(2)}) %collective-permute-start.1) | collective-permute-done | bytes 540704 | tf_op jit(solution)/shard_map/ppermute | solution.py:223
  259.7 31.3 %collective-permute-done.3 = f16[4,264,256]{2,1,0:T(8,128)(2,1)S(1)} collective-permute-done((f16[4,264,256]{2,1,0:T(8,128)(2,1)}, f16[4,264,256]{2,1,0:T(8,128)(2,1)S(1)}, u32[]{:S(2)}, u32[]{:S(2)}) %collective-permute-start.3) | collective-permute-done | bytes 540704 | tf_op jit(solution)/shard_map/ppermute | solution.py:223
  291.1 13.2 %collective-permute-done.4 = f16[4,264,256]{2,1,0:T(8,128)(2,1)S(1)} collective-permute-done((f16[4,264,256]{2,1,0:T(8,128)(2,1)S(1)}, f16[4,264,256]{2,1,0:T(8,128)(2,1)S(1)}, u32[]{:S(2)}, u32[]{:S(2)}) %collective-permute-start.4) | collective-permute-done | bytes 540704 | tf_op jit(solution)/shard_map/ppermute | solution.py:223
  304.5 9.5 %collective-permute-done.6 = f16[4,264,256]{2,1,0:T(8,128)(2,1)S(1)} collective-permute-done((f16[4,264,256]{2,1,0:T(8,128)(2,1)S(1)}, f16[4,264,256]{2,1,0:T(8,128)(2,1)S(1)}, u32[]{:S(2)}, u32[]{:S(2)}) %collective-permute-start.6) | collective-permute-done | bytes 540704 | tf_op jit(solution)/shard_map/ppermute | solution.py:223
  316.1 9.0 %shard_map.124 = f32[16,264,256]{2,1,0:T(8,128)} custom-call(bf16[8,16,32,512]{3,2,1,0:T(8,128)(2,1)} %all-to-all-done.2.spectra_ref), custom_call_target="tpu_custom_call" | custom-call | flops 2147483648 | bytes 8388608 | tf_op jit(solution)/shard_map/pallas_call | solution.py:107
  334.0 9.0 %shard_map.126 = f32[16,264,256]{2,1,0:T(8,128)} custom-call(bf16[8,16,32,512]{3,2,1,0:T(8,128)(2,1)} %all-to-all-done.3.spectra_ref), custom_call_target="tpu_custom_call" | custom-call | flops 2147483648 | bytes 8388608 | tf_op jit(solution)/shard_map/pallas_call | solution.py:107
  353.2 14.8 %collective-permute-done.8 = f16[4,264,256]{2,1,0:T(8,128)(2,1)} collective-permute-done((f16[4,264,256]{2,1,0:T(8,128)(2,1)}, f16[4,264,256]{2,1,0:T(8,128)(2,1)}, u32[]{:S(2)}, u32[]{:S(2)}) %collective-permute-start.8) | collective-permute-done | bytes 540704 | tf_op jit(solution)/shard_map/ppermute | solution.py:223
  369.2 32.4 %collective-permute-done.9 = f16[4,264,256]{2,1,0:T(8,128)(2,1)} collective-permute-done((f16[4,264,256]{2,1,0:T(8,128)(2,1)}, f16[4,264,256]{2,1,0:T(8,128)(2,1)}, u32[]{:S(2)}, u32[]{:S(2)}) %collective-permute-start.9) | collective-permute-done | bytes 540704 | tf_op jit(solution)/shard_map/ppermute | solution.py:223
  402.8 11.9 %collective-permute-done.10 = f16[4,264,256]{2,1,0:T(8,128)(2,1)S(1)} collective-permute-done((f16[4,264,256]{2,1,0:T(8,128)(2,1)S(1)}, f16[4,264,256]{2,1,0:T(8,128)(2,1)S(1)}, u32[]{:S(2)}, u32[]{:S(2)}) %collective-permute-start.10) | collective-permute-done | bytes 540704 | tf_op jit(solution)/shard_map/ppermute | solution.py:223
  415.5 9.1 %collective-permute-done.12 = f16[4,264,256]{2,1,0:T(8,128)(2,1)S(1)} collective-permute-done((f16[4,264,256]{2,1,0:T(8,128)(2,1)S(1)}, f16[4,264,256]{2,1,0:T(8,128)(2,1)S(1)}, u32[]{:S(2)}, u32[]{:S(2)}) %collective-permute-start.12) | collective-permute-done | bytes 540704 | tf_op jit(solution)/shard_map/ppermute | solution.py:223
  (81 shorter events, 56.7 us)
Async XLA Ops:
  0.9 8.5 %collective-permute-start = (bf16[32,3072]{1,0:T(8,128)(2,1)S(1)}, bf16[32,3072]{1,0:T(8,128)(2,1)S(1)}, u32[]{:S(2)}, u32[]{:S(2)}) collective-permute-start(bf16[32,3072]{1,0:T(8,128)(2,1)S(1)} %slice.143), channel_id=1, source_target_pairs={{0,1},{1,2},{2,3},{4,5},{5,6},{6,7},{8,9},{9,10},{10,11},{12,13},{... | collective-permute-start | bytes 589832 | tf_op jit(solution)/shard_map/ppermute | solution.py:20
  50.4 52.7 %all-to-all-start = ((bf16[8,16,32,512]{3,2,1,0:T(8,128)(2,1)}), bf16[8,16,32,512]{3,2,1,0:T(8,128)(2,1)}, u32[]{:S(2)}, u32[]{:S(2)}) async-start(bf16[8,16,32,512]{3,2,1,0:T(8,128)(2,1)} %bitcast.47), calls=%async_computation | async-start | bytes 8388608 | tf_op jit(solution)/shard_map/all_to_all | solution.py:212
  103.1 53.7 %all-to-all-start.1 = ((bf16[8,16,32,512]{3,2,1,0:T(8,128)(2,1)}), bf16[8,16,32,512]{3,2,1,0:T(8,128)(2,1)}, u32[]{:S(2)}, u32[]{:S(2)}) async-start(bf16[8,16,32,512]{3,2,1,0:T(8,128)(2,1)} %bitcast.46), calls=%async_computation.1 | async-start | bytes 8388608 | tf_op jit(solution)/shard_map/all_to_all | solution.py:212
  156.9 53.7 %all-to-all-start.2 = ((bf16[8,16,32,512]{3,2,1,0:T(8,128)(2,1)}), bf16[8,16,32,512]{3,2,1,0:T(8,128)(2,1)}, u32[]{:S(2)}, u32[]{:S(2)}) async-start(bf16[8,16,32,512]{3,2,1,0:T(8,128)(2,1)} %bitcast.45), calls=%async_computation.2 | async-start | bytes 8388608 | tf_op jit(solution)/shard_map/all_to_all | solution.py:212
  210.6 123.4 %all-to-all-start.3 = ((bf16[8,16,32,512]{3,2,1,0:T(8,128)(2,1)}), bf16[8,16,32,512]{3,2,1,0:T(8,128)(2,1)}, u32[]{:S(2)}, u32[]{:S(2)}) async-start(bf16[8,16,32,512]{3,2,1,0:T(8,128)(2,1)} %bitcast.44), calls=%async_computation.3 | async-start | bytes 8388608 | tf_op jit(solution)/shard_map/all_to_all | solution.py:212
  219.4 38.8 %copy-start.3 = (f32[4,264,256]{2,1,0:T(8,128)}, f32[4,264,256]{2,1,0:T(8,128)S(1)}, u32[]{:S(2)}) copy-start(f32[4,264,256]{2,1,0:T(8,128)S(1)} %get-tuple-element.13) | copy-start | bytes 3244036
  219.4 38.7 %collective-permute-start.1 = (f16[4,264,256]{2,1,0:T(8,128)(2,1)}, f16[4,264,256]{2,1,0:T(8,128)(2,1)}, u32[]{:S(2)}, u32[]{:S(2)}) collective-permute-start(f16[4,264,256]{2,1,0:T(8,128)(2,1)} %get-tuple-element.16), channel_id=1, source_target_pairs={{0,1},{1,2},{2,3},{3,0},{4,5},{5,6},{6,7},{7,4},{8,9},{9,10},{10,1... | collective-permute-start | bytes 1622024 | tf_op jit(solution)/shard_map/ppermute | solution.py:223
  221.0 38.6 %collective-permute-start.2 = (f16[4,264,256]{2,1,0:T(8,128)(2,1)}, f16[4,264,256]{2,1,0:T(8,128)(2,1)S(1)}, u32[]{:S(2)}, u32[]{:S(2)}) collective-permute-start(f16[4,264,256]{2,1,0:T(8,128)(2,1)} %get-tuple-element.15), channel_id=1, source_target_pairs={{0,2},{1,3},{2,0},{3,1},{4,6},{5,7},{6,4},{7,5},{8,10},{9,11},{10,... | collective-permute-start | bytes 1622024 | tf_op jit(solution)/shard_map/ppermute | solution.py:223
  221.4 36.7 %copy-start.7 = (s32[64]{0:T(128)S(1)}, s32[64]{0:T(128)}, u32[]{:S(2)}) copy-start(s32[64]{0:T(128)} %param.15) | copy-start | bytes 772
  221.4 69.7 %collective-permute-start.3 = (f16[4,264,256]{2,1,0:T(8,128)(2,1)}, f16[4,264,256]{2,1,0:T(8,128)(2,1)S(1)}, u32[]{:S(2)}, u32[]{:S(2)}) collective-permute-start(f16[4,264,256]{2,1,0:T(8,128)(2,1)} %get-tuple-element.14), channel_id=1, source_target_pairs={{0,3},{1,0},{2,1},{3,2},{4,7},{5,4},{6,5},{7,6},{8,11},{9,8},{10,9... | collective-permute-start | bytes 1622024 | tf_op jit(solution)/shard_map/ppermute | solution.py:223
  222.9 35.5 %copy-start = (f32[4,264,256]{2,1,0:T(8,128)}, f32[4,264,256]{2,1,0:T(8,128)S(1)}, u32[]{:S(2)}) copy-start(f32[4,264,256]{2,1,0:T(8,128)S(1)} %get-tuple-element.17) | copy-start | bytes 3244036
  222.9 81.4 %collective-permute-start.4 = (f16[4,264,256]{2,1,0:T(8,128)(2,1)S(1)}, f16[4,264,256]{2,1,0:T(8,128)(2,1)S(1)}, u32[]{:S(2)}, u32[]{:S(2)}) collective-permute-start(f16[4,264,256]{2,1,0:T(8,128)(2,1)S(1)} %get-tuple-element.20), channel_id=1, source_target_pairs={{0,1},{1,2},{2,3},{3,0},{4,5},{5,6},{6,7},{7,4},{8,9},{9,10},{10,1... | collective-permute-start | bytes 1622024 | tf_op jit(solution)/shard_map/ppermute | solution.py:223
  223.9 80.6 %collective-permute-start.5 = (f16[4,264,256]{2,1,0:T(8,128)(2,1)S(1)}, f16[4,264,256]{2,1,0:T(8,128)(2,1)S(1)}, u32[]{:S(2)}, u32[]{:S(2)}) collective-permute-start(f16[4,264,256]{2,1,0:T(8,128)(2,1)S(1)} %get-tuple-element.19), channel_id=1, source_target_pairs={{0,2},{1,3},{2,0},{3,1},{4,6},{5,7},{6,4},{7,5},{8,10},{9,11},{10,... | collective-permute-start | bytes 1622024 | tf_op jit(solution)/shard_map/ppermute | solution.py:223
  258.1 55.9 %collective-permute-start.6 = (f16[4,264,256]{2,1,0:T(8,128)(2,1)S(1)}, f16[4,264,256]{2,1,0:T(8,128)(2,1)S(1)}, u32[]{:S(2)}, u32[]{:S(2)}) collective-permute-start(f16[4,264,256]{2,1,0:T(8,128)(2,1)S(1)} %get-tuple-element.18), channel_id=1, source_target_pairs={{0,3},{1,0},{2,1},{3,2},{4,7},{5,4},{6,5},{7,6},{8,11},{9,8},{10,9... | collective-permute-start | bytes 1622024 | tf_op jit(solution)/shard_map/ppermute | solution.py:223
  304.5 10.3 %copy-start.4 = (f32[4,264,256]{2,1,0:T(8,128)S(1)}, f32[4,264,256]{2,1,0:T(8,128)}, u32[]{:S(2)}) copy-start(f32[4,264,256]{2,1,0:T(8,128)} %copy-done.3) | copy-start | bytes 3244036
  329.4 21.5 %collective-permute-start.7 = (f16[4,264,256]{2,1,0:T(8,128)(2,1)}, f16[4,264,256]{2,1,0:T(8,128)(2,1)}, u32[]{:S(2)}, u32[]{:S(2)}) collective-permute-start(f16[4,264,256]{2,1,0:T(8,128)(2,1)} %get-tuple-element.24), channel_id=1, source_target_pairs={{0,1},{1,2},{2,3},{3,0},{4,5},{5,6},{6,7},{7,4},{8,9},{9,10},{10,1... | collective-permute-start | bytes 1622024 | tf_op jit(solution)/shard_map/ppermute | solution.py:223
  332.5 35.6 %collective-permute-start.8 = (f16[4,264,256]{2,1,0:T(8,128)(2,1)}, f16[4,264,256]{2,1,0:T(8,128)(2,1)}, u32[]{:S(2)}, u32[]{:S(2)}) collective-permute-start(f16[4,264,256]{2,1,0:T(8,128)(2,1)} %get-tuple-element.23), channel_id=1, source_target_pairs={{0,2},{1,3},{2,0},{3,1},{4,6},{5,7},{6,4},{7,5},{8,10},{9,11},{10,... | collective-permute-start | bytes 1622024 | tf_op jit(solution)/shard_map/ppermute | solution.py:223
  333.3 68.3 %collective-permute-start.9 = (f16[4,264,256]{2,1,0:T(8,128)(2,1)}, f16[4,264,256]{2,1,0:T(8,128)(2,1)}, u32[]{:S(2)}, u32[]{:S(2)}) collective-permute-start(f16[4,264,256]{2,1,0:T(8,128)(2,1)} %get-tuple-element.22), channel_id=1, source_target_pairs={{0,3},{1,0},{2,1},{3,2},{4,7},{5,4},{6,5},{7,6},{8,11},{9,8},{10,9... | collective-permute-start | bytes 1622024 | tf_op jit(solution)/shard_map/ppermute | solution.py:223
  345.4 4.0 copy-start.1
  345.9 68.8 %collective-permute-start.10 = (f16[4,264,256]{2,1,0:T(8,128)(2,1)S(1)}, f16[4,264,256]{2,1,0:T(8,128)(2,1)S(1)}, u32[]{:S(2)}, u32[]{:S(2)}) collective-permute-start(f16[4,264,256]{2,1,0:T(8,128)(2,1)S(1)} %get-tuple-element.28), channel_id=1, source_target_pairs={{0,1},{1,2},{2,3},{3,0},{4,5},{5,6},{6,7},{7,4},{8,9},{9,10},{10,1... | collective-permute-start | bytes 1622024 | tf_op jit(solution)/shard_map/ppermute | solution.py:223
  347.3 67.5 %collective-permute-start.11 = (f16[4,264,256]{2,1,0:T(8,128)(2,1)S(1)}, f16[4,264,256]{2,1,0:T(8,128)(2,1)S(1)}, u32[]{:S(2)}, u32[]{:S(2)}) collective-permute-start(f16[4,264,256]{2,1,0:T(8,128)(2,1)S(1)} %get-tuple-element.27), channel_id=1, source_target_pairs={{0,2},{1,3},{2,0},{3,1},{4,6},{5,7},{6,4},{7,5},{8,10},{9,11},{10,... | collective-permute-start | bytes 1622024 | tf_op jit(solution)/shard_map/ppermute | solution.py:223
  349.4 1.2 copy-start.2
  350.9 73.7 %collective-permute-start.12 = (f16[4,264,256]{2,1,0:T(8,128)(2,1)S(1)}, f16[4,264,256]{2,1,0:T(8,128)(2,1)S(1)}, u32[]{:S(2)}, u32[]{:S(2)}) collective-permute-start(f16[4,264,256]{2,1,0:T(8,128)(2,1)S(1)} %get-tuple-element.26), channel_id=1, source_target_pairs={{0,3},{1,0},{2,1},{3,2},{4,7},{5,4},{6,5},{7,6},{8,11},{9,8},{10,9... | collective-permute-start | bytes 1622024 | tf_op jit(solution)/shard_map/ppermute | solution.py:223
  425.2 1.2 copy-start.5
  (1 other events, 0.7 us)

commit v3 on v2

--- a/solution.py
+++ b/solution.py
@@ -69,7 +69,7 @@
         scratch_shapes=[pltpu.VMEM((rows * inputs, 128), jnp.float32)] * (2 * frames // 128),
         compiler_params=pltpu.CompilerParams(vmem_limit_bytes=VMEM_LIMIT),
         cost_estimate=pl.CostEstimate(
-            flops=4 * rows * inputs_here * frames * fft_length,
+            flops=10 * 4 * rows * inputs_here * frames * fft_length,
             bytes_accessed=2 * inputs_here * frames * (fft_length + 2 * rows),
             transcendentals=0,
         ),
@@ -112,7 +112,7 @@
         out_specs=pl.BlockSpec((step, total + EXTRA_ROWS, total), lambda b: (b, 0, 0)),
         compiler_params=pltpu.CompilerParams(vmem_limit_bytes=VMEM_LIMIT),
         cost_estimate=pl.CostEstimate(
-            flops=4 * channels * total * total * columns,
+            flops=40 * 4 * channels * total * total * columns,
             bytes_accessed=2 * channels * total * (columns + 2 * total),
             transcendentals=0,
         ),
@@ -195,9 +195,24 @@
     local_flags = lax.dynamic_slice_in_dim(
         channel_flags, lax.axis_index("tm") * kept, kept, 0
     ).astype(jnp.float32)
+    flag_parts = (local_flags * (1.0 / (SEND_PEAK * frame_total))).reshape(chunks, width)
     scale = 1.0 / math.sqrt(fft_length)
     order = np.arange(feeds * owned).reshape(feeds, times, chunks, width)
     place = lax.axis_index("tm")
+
+    def summed(vis, flags):
+        total = 0.0
+        for shift in range(times):
+            target = lax.rem(place + shift, times)
+            part = lax.dynamic_index_in_dim(vis, target, 0, keepdims=False)
+            if shift:
+                route = [(i, (i + shift) % times) for i in range(times)]
+                part = lax.ppermute(part, "tm", route)
+            part = part.astype(jnp.float32)
+            count = part.shape[2]
+            total = total + part[:, :count] * jnp.exp2(part[:, count:, :1][:, :1])
+        return total * flags[:, None, None]
+
     results = []
     sent = []
     for k in range(chunks):
@@ -207,24 +222,18 @@
         angles = angles * delays.reshape(-1, 1, block)
         if k >= 2:
             filtered, sent[k - 2] = lax.optimization_barrier((filtered, sent[k - 2]))
+            results.append(summed(sent[k - 2], flag_parts[k - 2]))
         spectra = dft_call(table, jnp.cos(angles) * scale, jnp.sin(angles) * scale, filtered)
         spectra = spectra.reshape(feeds, times * width, inputs_here, spectra.shape[2])
+        if k >= 3:
+            spectra, results[k - 3] = lax.optimization_barrier((spectra, results[k - 3]))
         turned = lax.all_to_all(spectra, "feed", split_axis=0, concat_axis=0, tiled=True)
+        if k >= 2:
+            turned, results[k - 2] = lax.optimization_barrier((turned, results[k - 2]))
         vis = gram_call(turned).astype(jnp.float16)
         sent.append(vis.reshape(times, width, vis.shape[1], vis.shape[2]))
-    for k in range(chunks):
-        flags = local_flags[k * width : (k + 1) * width] * (1.0 / (SEND_PEAK * frame_total))
-        total = 0.0
-        for shift in range(times):
-            target = lax.rem(place + shift, times)
-            part = lax.dynamic_index_in_dim(sent[k], target, 0, keepdims=False)
-            if shift:
-                route = [(i, (i + shift) % times) for i in range(times)]
-                part = lax.ppermute(part, "tm", route)
-            part = part.astype(jnp.float32)
-            count = part.shape[2]
-            total = total + part[:, :count] * jnp.exp2(part[:, count:, :1][:, :1])
-        results.append(total * flags[:, None, None])
+    for k in range(len(results), chunks):
+        results.append(summed(sent[k], flag_parts[k]))
     return jnp.concatenate(results, axis=0)
 
 

time: 433 us -> 362 us (0.84)
  waiting for transfers between devices: 232 us -> 166 us
    ppermute x12, waiting for transfers between devices: 154 us -> 114 us  [summed(): part = lax.ppermute(part, 'tm', route)]
    all_to_all x4, waiting for transfers between devices: 77.2 us -> 51.4 us  [on_device(): lax.all_to_all(spectra, 'feed', split_axis=0, concat_axis=0, tiled=True)]
    convert_element_type x17 -> x16, other arithmetic: 10.7 us -> 6.89 us  [summed(): part = part.astype(jnp.float32)]
  transfers between devices with their start and end apart: 17 -> 17, of which waited for: 12 -> 10; matrix products, arithmetic and copies ran while one was open for 7% -> 7% of each run, Pallas kernels for 18% -> 19%
where the time goes in v3:
time: 362 us; the launch traced here: 357 us
  waiting for transfers between devices  166 us (46%)
  Pallas kernels  118 us (33%)
  starting transfers between devices  40.2 us (11%)
  other arithmetic  29.3 us (8%)
  local copies, waits for them, and re-layouts  4.23 us (1%)
    ppermute x12, waiting for transfers between devices, summed(): part = lax.ppermute(part, 'tm', route)  114 us
    pallas_call x4, Pallas kernels, dft_call(): pl.pallas_call(dft_kernel, out_shape=out_shape, grid=(blocks,), in_specs=...  55.6 us
    all_to_all x4, waiting for transfers between devices, on_device(): lax.all_to_all(spectra, 'feed', split_axis=0, concat_axis=0, tiled=True)  51.4 us
    pallas_call x4, Pallas kernels, gram_call(): pl.pallas_call(gram_kernel, out_shape=jax.ShapeDtypeStruct((channels, tot...  35.9 us
    pallas_call x1, Pallas kernels, filter_frames(): pl.pallas_call(filter_kernel, out_shape=jax.ShapeDtypeStruct((inputs_here...  26.4 us
    all_to_all x4, starting transfers between devices, on_device(): lax.all_to_all(spectra, 'feed', split_axis=0, concat_axis=0, tiled=True)  21.7 us
    ppermute x12, starting transfers between devices, summed(): part = lax.ppermute(part, 'tm', route)  15 us
    convert_element_type x4, other arithmetic, on_device(): vis = gram_call(turned).astype(jnp.float16)  10 us
  transfers between devices with their start and end apart: 17, of which 10 were waited for; matrix products, arithmetic and copies ran while one was open for 7% of the time, Pallas kernels for 19%

profile of v3, /device:TPU:18, one launch (start us, length us, event | category | flops | bytes accessed | tf_op | source)
XLA Modules:
  0.0 357.4 jit_solution(2559480966817171685)
XLA Ops:
  5.9 3.9 %fusion.23 = (f32[2,128,16]{2,1,0:T(8,128)}, f32[2,128,16]{2,1,0:T(8,128)}, f32[2,128,16]{2,1,0:T(8,128)}, f32[2,128,16]{2,1,0:T(8,128)}, f32[2,128,16]{2,1,0:T(...) fusion(f32[128]{0:T(128)} %constant.95, f32[2,16]{1,0:T(2,128)S(1)} %mul.288, ...), kind=kLoop, calls=%fused_computation.64 | loop fusion | flops 49152 | bytes 133248 | tf_op jit(solution)/shard_map/mul | solution.py:226
  11.1 26.4 %shard_map.118.filtered_ref = bf16[32,256,1024]{2,1,0:T(8,128)(2,1)} custom-call(bf16[32,3072]{1,0:T(8,128)(2,1)} %copy-done.7, f32[4,1024]{1,0:T(4,128)} %taps_ref.1, bf16[32,262144]{1,0:T(8,128)(2,1)} %block_ref.1), custom_call_target="tpu_custom_call" | custom-call | flops 67108864 | bytes 33554432 | tf_op jit(solution)/shard_map/pallas_call | solution.py:160
  37.5 13.9 %shard_map.119 = bf16[128,32,512]{2,1,0:T(8,128)(2,1)} custom-call(bf16[256,1024]{1,0:T(8,128)(2,1)} %constant.84.clone.table_ref, f32[2,128,16]{2,1,0:T(8,128)} %get-tuple-element.51.cos_ref, f32[2,128,16]{2,1,0:T(8,128)} %get-tuple-element.52.sin_ref, bf16[32,256,1024]{2,1,0:T(8,128)(2,1)} %shard_map.118.filtered_ref), custom_call_target="tpu_custom_call" | custom-call | flops 42949672960 | bytes 20971520 | tf_op jit(solution)/shard_map/pallas_call | solution.py:58
  51.4 5.0 %all-to-all-start = ((bf16[8,16,32,512]{3,2,1,0:T(8,128)(2,1)}), bf16[8,16,32,512]{3,2,1,0:T(8,128)(2,1)}, u32[]{:S(2)}, u32[]{:S(2)}) async-start(bf16[8,16,32,512]{3,2,1,0:T(8,128)(2,1)} %bitcast.51), calls=%async_computation | async-start | bytes 8388608 | tf_op jit(solution)/shard_map/all_to_all | solution.py:230
  56.4 13.9 %shard_map.121 = bf16[128,32,512]{2,1,0:T(8,128)(2,1)} custom-call(bf16[256,1024]{1,0:T(8,128)(2,1)} %constant.86.clone.table_ref, f32[2,128,16]{2,1,0:T(8,128)} %get-tuple-element.49.cos_ref, f32[2,128,16]{2,1,0:T(8,128)} %get-tuple-element.50.sin_ref, bf16[32,256,1024]{2,1,0:T(8,128)(2,1)} %shard_map.118.filtered_ref), custom_call_target="tpu_custom_call" | custom-call | flops 42949672960 | bytes 20971520 | tf_op jit(solution)/shard_map/pallas_call | solution.py:58
  70.3 33.9 %all-to-all-done.spectra_ref = bf16[8,16,32,512]{3,2,1,0:T(8,128)(2,1)} async-done(((bf16[8,16,32,512]{3,2,1,0:T(8,128)(2,1)}), bf16[8,16,32,512]{3,2,1,0:T(8,128)(2,1)}, u32[]{:S(2)}, u32[]{:S(2)}) %all-to-all-start) | async-done | bytes 4194336 | tf_op jit(solution)/shard_map/all_to_all | solution.py:230
  104.1 6.0 %all-to-all-start.1 = ((bf16[8,16,32,512]{3,2,1,0:T(8,128)(2,1)}), bf16[8,16,32,512]{3,2,1,0:T(8,128)(2,1)}, u32[]{:S(2)}, u32[]{:S(2)}) async-start(bf16[8,16,32,512]{3,2,1,0:T(8,128)(2,1)} %bitcast.50), calls=%async_computation.1 | async-start | bytes 8388608 | tf_op jit(solution)/shard_map/all_to_all | solution.py:230
  110.1 9.0 %shard_map.120 = f32[16,264,256]{2,1,0:T(8,128)} custom-call(bf16[8,16,32,512]{3,2,1,0:T(8,128)(2,1)} %all-to-all-done.spectra_ref), custom_call_target="tpu_custom_call" | custom-call | flops 85899345920 | bytes 8388608 | tf_op jit(solution)/shard_map/pallas_call | solution.py:107
  126.4 13.9 %shard_map.124 = bf16[128,32,512]{2,1,0:T(8,128)(2,1)} custom-call(bf16[256,1024]{1,0:T(8,128)(2,1)} %constant.88.clone.table_ref, f32[2,128,16]{2,1,0:T(8,128)} %get-tuple-element.42.cos_ref, f32[2,128,16]{2,1,0:T(8,128)} %get-tuple-element.41.sin_ref, bf16[32,256,1024]{2,1,0:T(8,128)(2,1)} %shard_map.118.filtered_ref), custom_call_target="tpu_custom_call" | custom-call | flops 42949672960 | bytes 20971520 | tf_op jit(solution)/shard_map/pallas_call | solution.py:58
  140.3 17.5 %all-to-all-done.1.spectra_ref = bf16[8,16,32,512]{3,2,1,0:T(8,128)(2,1)} async-done(((bf16[8,16,32,512]{3,2,1,0:T(8,128)(2,1)}), bf16[8,16,32,512]{3,2,1,0:T(8,128)(2,1)}, u32[]{:S(2)}, u32[]{:S(2)}) %all-to-all-start.1) | async-done | bytes 4194336 | tf_op jit(solution)/shard_map/all_to_all | solution.py:230
  157.8 6.0 %all-to-all-start.2 = ((bf16[8,16,32,512]{3,2,1,0:T(8,128)(2,1)}), bf16[8,16,32,512]{3,2,1,0:T(8,128)(2,1)}, u32[]{:S(2)}, u32[]{:S(2)}) async-start(bf16[8,16,32,512]{3,2,1,0:T(8,128)(2,1)} %bitcast.49), calls=%async_computation.2 | async-start | bytes 8388608 | tf_op jit(solution)/shard_map/all_to_all | solution.py:230
  163.8 9.0 %shard_map.122 = f32[16,264,256]{2,1,0:T(8,128)} custom-call(bf16[8,16,32,512]{3,2,1,0:T(8,128)(2,1)} %all-to-all-done.1.spectra_ref), custom_call_target="tpu_custom_call" | custom-call | flops 85899345920 | bytes 8388608 | tf_op jit(solution)/shard_map/pallas_call | solution.py:107
  179.0 13.9 %shard_map.123 = bf16[128,32,512]{2,1,0:T(8,128)(2,1)} custom-call(bf16[256,1024]{1,0:T(8,128)(2,1)} %constant.90.clone.table_ref, f32[2,128,16]{2,1,0:T(8,128)} %get-tuple-element.53.cos_ref, f32[2,128,16]{2,1,0:T(8,128)} %get-tuple-element.54.sin_ref, bf16[32,256,1024]{2,1,0:T(8,128)(2,1)} %shard_map.118.filtered_ref), custom_call_target="tpu_custom_call" | custom-call | flops 42949672960 | bytes 20971520 | tf_op jit(solution)/shard_map/pallas_call | solution.py:58
  195.6 18.5 %collective-permute-done.4 = f16[4,264,256]{2,1,0:T(8,128)(2,1)S(1)} collective-permute-done((f16[4,264,256]{2,1,0:T(8,128)(2,1)S(1)}, f16[4,264,256]{2,1,0:T(8,128)(2,1)S(1)}, u32[]{:S(2)}, u32[]{:S(2)}) %collective-permute-start.4) | collective-permute-done | bytes 540704 | tf_op jit(solution)/shard_map/ppermute | solution.py:210
  214.2 9.4 %collective-permute-done.6 = f16[4,264,256]{2,1,0:T(8,128)(2,1)} collective-permute-done((f16[4,264,256]{2,1,0:T(8,128)(2,1)S(1)}, f16[4,264,256]{2,1,0:T(8,128)(2,1)}, u32[]{:S(2)}, u32[]{:S(2)}) %collective-permute-start.6) | collective-permute-done | bytes 540704 | tf_op jit(solution)/shard_map/ppermute | solution.py:210
  226.8 4.8 %all-to-all-start.3 = ((bf16[8,16,32,512]{3,2,1,0:T(8,128)(2,1)}), bf16[8,16,32,512]{3,2,1,0:T(8,128)(2,1)}, u32[]{:S(2)}, u32[]{:S(2)}) async-start(bf16[8,16,32,512]{3,2,1,0:T(8,128)(2,1)} %bitcast.48), calls=%async_computation.3 | async-start | bytes 8388608 | tf_op jit(solution)/shard_map/all_to_all | solution.py:230
  231.6 9.0 %shard_map.125 = f32[16,264,256]{2,1,0:T(8,128)} custom-call(bf16[8,16,32,512]{3,2,1,0:T(8,128)(2,1)} %all-to-all-done.2.spectra_ref), custom_call_target="tpu_custom_call" | custom-call | flops 85899345920 | bytes 8388608 | tf_op jit(solution)/shard_map/pallas_call | solution.py:107
  249.5 9.8 %collective-permute-done.7 = f16[4,264,256]{2,1,0:T(8,128)(2,1)S(1)} collective-permute-done((f16[4,264,256]{2,1,0:T(8,128)(2,1)S(1)}, f16[4,264,256]{2,1,0:T(8,128)(2,1)S(1)}, u32[]{:S(2)}, u32[]{:S(2)}) %collective-permute-start.7) | collective-permute-done | bytes 540704 | tf_op jit(solution)/shard_map/ppermute | solution.py:210
  259.4 21.9 %collective-permute-done.8 = f16[4,264,256]{2,1,0:T(8,128)(2,1)S(1)} collective-permute-done((f16[4,264,256]{2,1,0:T(8,128)(2,1)S(1)}, f16[4,264,256]{2,1,0:T(8,128)(2,1)S(1)}, u32[]{:S(2)}, u32[]{:S(2)}) %collective-permute-start.8) | collective-permute-done | bytes 540704 | tf_op jit(solution)/shard_map/ppermute | solution.py:210
  281.3 11.4 %collective-permute-done.9 = f16[4,264,256]{2,1,0:T(8,128)(2,1)S(1)} collective-permute-done((f16[4,264,256]{2,1,0:T(8,128)(2,1)S(1)}, f16[4,264,256]{2,1,0:T(8,128)(2,1)S(1)}, u32[]{:S(2)}, u32[]{:S(2)}) %collective-permute-start.9) | collective-permute-done | bytes 540704 | tf_op jit(solution)/shard_map/ppermute | solution.py:210
  293.1 9.0 %shard_map.126 = f32[16,264,256]{2,1,0:T(8,128)} custom-call(bf16[8,16,32,512]{3,2,1,0:T(8,128)(2,1)} %all-to-all-done.3.spectra_ref), custom_call_target="tpu_custom_call" | custom-call | flops 85899345920 | bytes 8388608 | tf_op jit(solution)/shard_map/pallas_call | solution.py:107
  309.7 11.3 %collective-permute-done.10 = f16[4,264,256]{2,1,0:T(8,128)(2,1)S(1)} collective-permute-done((f16[4,264,256]{2,1,0:T(8,128)(2,1)S(1)}, f16[4,264,256]{2,1,0:T(8,128)(2,1)S(1)}, u32[]{:S(2)}, u32[]{:S(2)}) %collective-permute-start.10) | collective-permute-done | bytes 540704 | tf_op jit(solution)/shard_map/ppermute | solution.py:210
  321.1 20.7 %collective-permute-done.11 = f16[4,264,256]{2,1,0:T(8,128)(2,1)S(1)} collective-permute-done((f16[4,264,256]{2,1,0:T(8,128)(2,1)S(1)}, f16[4,264,256]{2,1,0:T(8,128)(2,1)S(1)}, u32[]{:S(2)}, u32[]{:S(2)}) %collective-permute-start.11) | collective-permute-done | bytes 540704 | tf_op jit(solution)/shard_map/ppermute | solution.py:210
  342.1 11.2 %collective-permute-done.12 = f16[4,264,256]{2,1,0:T(8,128)(2,1)S(1)} collective-permute-done((f16[4,264,256]{2,1,0:T(8,128)(2,1)S(1)}, f16[4,264,256]{2,1,0:T(8,128)(2,1)S(1)}, u32[]{:S(2)}, u32[]{:S(2)}) %collective-permute-start.12) | collective-permute-done | bytes 540704 | tf_op jit(solution)/shard_map/ppermute | solution.py:210
  (89 shorter events, 48.2 us)
Async XLA Ops:
  0.9 9.5 %collective-permute-start = (bf16[32,3072]{1,0:T(8,128)(2,1)S(1)}, bf16[32,3072]{1,0:T(8,128)(2,1)S(1)}, u32[]{:S(2)}, u32[]{:S(2)}) collective-permute-start(bf16[32,3072]{1,0:T(8,128)(2,1)S(1)} %slice.147), channel_id=1, source_target_pairs={{0,1},{1,2},{2,3},{4,5},{5,6},{6,7},{8,9},{9,10},{10,11},{12,13},{... | collective-permute-start | bytes 589832 | tf_op jit(solution)/shard_map/ppermute | solution.py:20
  51.4 52.7 %all-to-all-start = ((bf16[8,16,32,512]{3,2,1,0:T(8,128)(2,1)}), bf16[8,16,32,512]{3,2,1,0:T(8,128)(2,1)}, u32[]{:S(2)}, u32[]{:S(2)}) async-start(bf16[8,16,32,512]{3,2,1,0:T(8,128)(2,1)} %bitcast.51), calls=%async_computation | async-start | bytes 8388608 | tf_op jit(solution)/shard_map/all_to_all | solution.py:230
  104.1 53.7 %all-to-all-start.1 = ((bf16[8,16,32,512]{3,2,1,0:T(8,128)(2,1)}), bf16[8,16,32,512]{3,2,1,0:T(8,128)(2,1)}, u32[]{:S(2)}, u32[]{:S(2)}) async-start(bf16[8,16,32,512]{3,2,1,0:T(8,128)(2,1)} %bitcast.50), calls=%async_computation.1 | async-start | bytes 8388608 | tf_op jit(solution)/shard_map/all_to_all | solution.py:230
  123.2 54.5 %collective-permute-start.1 = (f16[4,264,256]{2,1,0:T(8,128)(2,1)S(1)}, f16[4,264,256]{2,1,0:T(8,128)(2,1)S(1)}, u32[]{:S(2)}, u32[]{:S(2)}) collective-permute-start(f16[4,264,256]{2,1,0:T(8,128)(2,1)S(1)} %get-tuple-element.40), channel_id=1, source_target_pairs={{0,1},{1,2},{2,3},{3,0},{4,5},{5,6},{6,7},{7,4},{8,9},{9,10},{10,1... | collective-permute-start | bytes 1622024 | tf_op jit(solution)/shard_map/ppermute | solution.py:210
  123.7 69.5 %collective-permute-start.2 = (f16[4,264,256]{2,1,0:T(8,128)(2,1)}, f16[4,264,256]{2,1,0:T(8,128)(2,1)}, u32[]{:S(2)}, u32[]{:S(2)}) collective-permute-start(f16[4,264,256]{2,1,0:T(8,128)(2,1)} %get-tuple-element.39), channel_id=1, source_target_pairs={{0,2},{1,3},{2,0},{3,1},{4,6},{5,7},{6,4},{7,5},{8,10},{9,11},{10,... | collective-permute-start | bytes 1622024 | tf_op jit(solution)/shard_map/ppermute | solution.py:210
  125.1 69.4 %collective-permute-start.3 = (f16[4,264,256]{2,1,0:T(8,128)(2,1)}, f16[4,264,256]{2,1,0:T(8,128)(2,1)}, u32[]{:S(2)}, u32[]{:S(2)}) collective-permute-start(f16[4,264,256]{2,1,0:T(8,128)(2,1)} %get-tuple-element.38), channel_id=1, source_target_pairs={{0,3},{1,0},{2,1},{3,2},{4,7},{5,4},{6,5},{7,6},{8,11},{9,8},{10,9... | collective-permute-start | bytes 1622024 | tf_op jit(solution)/shard_map/ppermute | solution.py:210
  157.8 69.0 %all-to-all-start.2 = ((bf16[8,16,32,512]{3,2,1,0:T(8,128)(2,1)}), bf16[8,16,32,512]{3,2,1,0:T(8,128)(2,1)}, u32[]{:S(2)}, u32[]{:S(2)}) async-start(bf16[8,16,32,512]{3,2,1,0:T(8,128)(2,1)} %bitcast.49), calls=%async_computation.2 | async-start | bytes 8388608 | tf_op jit(solution)/shard_map/all_to_all | solution.py:230
  175.7 17.4 %copy-start = (f32[4,264,256]{2,1,0:T(8,128)}, f32[4,264,256]{2,1,0:T(8,128)S(1)}, u32[]{:S(2)}) copy-start(f32[4,264,256]{2,1,0:T(8,128)S(1)} %get-tuple-element.33) | copy-start | bytes 3244036
  175.7 38.3 %collective-permute-start.4 = (f16[4,264,256]{2,1,0:T(8,128)(2,1)S(1)}, f16[4,264,256]{2,1,0:T(8,128)(2,1)S(1)}, u32[]{:S(2)}, u32[]{:S(2)}) collective-permute-start(f16[4,264,256]{2,1,0:T(8,128)(2,1)S(1)} %get-tuple-element.36), channel_id=1, source_target_pairs={{0,1},{1,2},{2,3},{3,0},{4,5},{5,6},{6,7},{7,4},{8,9},{9,10},{10,1... | collective-permute-start | bytes 1622024 | tf_op jit(solution)/shard_map/ppermute | solution.py:210
  176.3 37.8 %collective-permute-start.5 = (f16[4,264,256]{2,1,0:T(8,128)(2,1)S(1)}, f16[4,264,256]{2,1,0:T(8,128)(2,1)S(1)}, u32[]{:S(2)}, u32[]{:S(2)}) collective-permute-start(f16[4,264,256]{2,1,0:T(8,128)(2,1)S(1)} %get-tuple-element.35), channel_id=1, source_target_pairs={{0,2},{1,3},{2,0},{3,1},{4,6},{5,7},{6,4},{7,5},{8,10},{9,11},{10,... | collective-permute-start | bytes 1622024 | tf_op jit(solution)/shard_map/ppermute | solution.py:210
  177.7 46.0 %collective-permute-start.6 = (f16[4,264,256]{2,1,0:T(8,128)(2,1)S(1)}, f16[4,264,256]{2,1,0:T(8,128)(2,1)}, u32[]{:S(2)}, u32[]{:S(2)}) collective-permute-start(f16[4,264,256]{2,1,0:T(8,128)(2,1)S(1)} %get-tuple-element.34), channel_id=1, source_target_pairs={{0,3},{1,0},{2,1},{3,2},{4,7},{5,4},{6,5},{7,6},{8,11},{9,8},{10,9... | collective-permute-start | bytes 1622024 | tf_op jit(solution)/shard_map/ppermute | solution.py:210
  179.0 13.9 %copy-start.2 = (f32[4,264,256]{2,1,0:T(8,128)S(1)}, f32[4,264,256]{2,1,0:T(8,128)}, u32[]{:S(2)}) copy-start(f32[4,264,256]{2,1,0:T(8,128)} %get-tuple-element.37) | copy-start | bytes 3244036
  214.2 11.2 %copy-start.11 = (f32[4]{0:T(128)S(1)}, f32[4]{0:T(128)}, u32[]{:S(2)}) copy-start(f32[4]{0:T(128)} %get-tuple-element.58) | copy-start | bytes 52
  226.8 66.3 %all-to-all-start.3 = ((bf16[8,16,32,512]{3,2,1,0:T(8,128)(2,1)}), bf16[8,16,32,512]{3,2,1,0:T(8,128)(2,1)}, u32[]{:S(2)}, u32[]{:S(2)}) async-start(bf16[8,16,32,512]{3,2,1,0:T(8,128)(2,1)} %bitcast.48), calls=%async_computation.3 | async-start | bytes 8388608 | tf_op jit(solution)/shard_map/all_to_all | solution.py:230
  243.1 4.9 %copy-start.1 = (f32[4,264,256]{2,1,0:T(8,128)S(1)}, f32[4,264,256]{2,1,0:T(8,128)}, u32[]{:S(2)}) copy-start(f32[4,264,256]{2,1,0:T(8,128)} %copy-done) | copy-start | bytes 3244036
  243.1 4.9 %copy-start.10 = (f32[4]{0:T(128)S(1)}, f32[4]{0:T(128)}, u32[]{:S(2)}) copy-start(f32[4]{0:T(128)} %get-tuple-element.57) | copy-start | bytes 52
  243.5 5.8 %copy-start.3 = (f32[4,264,256]{2,1,0:T(8,128)}, f32[4,264,256]{2,1,0:T(8,128)S(1)}, u32[]{:S(2)}) copy-start(f32[4,264,256]{2,1,0:T(8,128)S(1)} %get-tuple-element.25) | copy-start | bytes 3244036
  243.5 15.8 %collective-permute-start.7 = (f16[4,264,256]{2,1,0:T(8,128)(2,1)S(1)}, f16[4,264,256]{2,1,0:T(8,128)(2,1)S(1)}, u32[]{:S(2)}, u32[]{:S(2)}) collective-permute-start(f16[4,264,256]{2,1,0:T(8,128)(2,1)S(1)} %get-tuple-element.28), channel_id=1, source_target_pairs={{0,1},{1,2},{2,3},{3,0},{4,5},{5,6},{6,7},{7,4},{8,9},{9,10},{10,1... | collective-permute-start | bytes 1622024 | tf_op jit(solution)/shard_map/ppermute | solution.py:210
  246.4 34.9 %collective-permute-start.8 = (f16[4,264,256]{2,1,0:T(8,128)(2,1)S(1)}, f16[4,264,256]{2,1,0:T(8,128)(2,1)S(1)}, u32[]{:S(2)}, u32[]{:S(2)}) collective-permute-start(f16[4,264,256]{2,1,0:T(8,128)(2,1)S(1)} %get-tuple-element.27), channel_id=1, source_target_pairs={{0,2},{1,3},{2,0},{3,1},{4,6},{5,7},{6,4},{7,5},{8,10},{9,11},{10,... | collective-permute-start | bytes 1622024 | tf_op jit(solution)/shard_map/ppermute | solution.py:210
  247.6 45.1 %collective-permute-start.9 = (f16[4,264,256]{2,1,0:T(8,128)(2,1)S(1)}, f16[4,264,256]{2,1,0:T(8,128)(2,1)S(1)}, u32[]{:S(2)}, u32[]{:S(2)}) collective-permute-start(f16[4,264,256]{2,1,0:T(8,128)(2,1)S(1)} %get-tuple-element.26), channel_id=1, source_target_pairs={{0,3},{1,0},{2,1},{3,2},{4,7},{5,4},{6,5},{7,6},{8,11},{9,8},{10,9... | collective-permute-start | bytes 1622024 | tf_op jit(solution)/shard_map/ppermute | solution.py:210
  305.0 16.0 %collective-permute-start.10 = (f16[4,264,256]{2,1,0:T(8,128)(2,1)S(1)}, f16[4,264,256]{2,1,0:T(8,128)(2,1)S(1)}, u32[]{:S(2)}, u32[]{:S(2)}) collective-permute-start(f16[4,264,256]{2,1,0:T(8,128)(2,1)S(1)} %get-tuple-element.32), channel_id=1, source_target_pairs={{0,1},{1,2},{2,3},{3,0},{4,5},{5,6},{6,7},{7,4},{8,9},{9,10},{10,1... | collective-permute-start | bytes 1622024 | tf_op jit(solution)/shard_map/ppermute | solution.py:210
  307.4 34.4 %collective-permute-start.11 = (f16[4,264,256]{2,1,0:T(8,128)(2,1)S(1)}, f16[4,264,256]{2,1,0:T(8,128)(2,1)S(1)}, u32[]{:S(2)}, u32[]{:S(2)}) collective-permute-start(f16[4,264,256]{2,1,0:T(8,128)(2,1)S(1)} %get-tuple-element.31), channel_id=1, source_target_pairs={{0,2},{1,3},{2,0},{3,1},{4,6},{5,7},{6,4},{7,5},{8,10},{9,11},{10,... | collective-permute-start | bytes 1622024 | tf_op jit(solution)/shard_map/ppermute | solution.py:210
  309.1 44.2 %collective-permute-start.12 = (f16[4,264,256]{2,1,0:T(8,128)(2,1)S(1)}, f16[4,264,256]{2,1,0:T(8,128)(2,1)S(1)}, u32[]{:S(2)}, u32[]{:S(2)}) collective-permute-start(f16[4,264,256]{2,1,0:T(8,128)(2,1)S(1)} %get-tuple-element.30), channel_id=1, source_target_pairs={{0,3},{1,0},{2,1},{3,2},{4,7},{5,4},{6,5},{7,6},{8,11},{9,8},{10,9... | collective-permute-start | bytes 1622024 | tf_op jit(solution)/shard_map/ppermute | solution.py:210
  341.9 11.6 %copy-start.8 = (f32[4]{0:T(128)S(1)}, f32[4]{0:T(128)}, u32[]{:S(2)}) copy-start(f32[4]{0:T(128)} %get-tuple-element.56) | copy-start | bytes 52
  (5 other events, 12.7 us)
